TPU v7x, 512 devices: a whole 4x4x16 slice. The times are simulated.
512 devices in a mesh: px: 16 (over z), py: 32 (over y, x, core).
Axes of the slice: x: 4, y: 4, z: 16, core: 2. Of those that a mesh axis runs over, the one named last changes fastest.
Arguments:
- displacement: float32 [6, 128, 4096], P(None, 'px', 'py'), may hold values from -6 to 6
- velocity: float32 [6, 128, 4096], P(None, 'px', 'py'), may hold values from -6 to 6
- external_force: float32 [6, 128, 4096], P(None, 'px', 'py')
- lumped_mass: float32 [128, 4096], P('px', 'py'), may hold values from 0.5 to 2
- thickness: float32 [128, 4096], P('px', 'py')
- added_mass: float32 [128, 4096], P('px', 'py'), may hold values from 0.5 to 4
- stiffness: float32 [24, 24], replicated, as said below
- elements: int32 [160, 4096], P('px', 'py'), may hold values from 0 to 1168, as said below
- counts: int32 [16, 32], P('px', 'py'), may hold values from 1 to 1161
Outputs:
- new_velocity: float32 [6, 128, 4096], P(None, 'px', 'py')
- new_displacement: float32 [6, 128, 4096], P(None, 'px', 'py')
Inputs may be any that keep to these rules, and one draw needn't show every extreme that they name: Each partition lists every element that touches one of its nodes, lies wholly inside the grid and is live, first and in some order, then the other elements of its extended block and zeros; an element is live for all partitions that list it or for none. `stiffness`: symmetric.
All inputs are finite; a program needn't handle non-finite values.
Results may differ from a plain program's by a relative error of at most 0.0003.
Values sent between devices are 32-bit elements; how exact they have to be, the bound alone decides.
A program may use at most 64 MiB of HBM per device.

v0:
```python
import jax
import jax.numpy as jnp
from jax import lax
from jax.sharding import PartitionSpec as P

ITERS = 4


highest = lax.Precision.HIGHEST


def extended_2(array, sides, width):
    for axis, dim in sides:
        peers, length = (lax.axis_size(axis), array.shape[dim])
        up = [(i, (i + 1) % peers) for i in range(peers - 1)]
        down = [(j, i) for i, j in up]
        last = lax.slice_in_dim(array, length - width, length, axis=dim)
        first = lax.slice_in_dim(array, 0, width, axis=dim)
        before = lax.ppermute(last, axis, up)
        after = lax.ppermute(first, axis, down)
        array = jnp.concatenate([before, array, after], axis=dim)
    return array


def corner_nodes(element_ids, stride):
    return jnp.stack([element_ids, element_ids + 1, element_ids + stride, element_ids + stride + 1])


def assemble(extended, element_ids, weight, kernel, stride):
    summed = jnp.zeros(extended.shape, jnp.float32)
    corners = corner_nodes(element_ids, stride)
    values = kernel(extended[:, corners], weight)
    return summed.at[:, corners.reshape(-1)].add(values.reshape(extended.shape[0], -1))


def mass_kernel(gathered, weight):
    return (gathered - jnp.mean(gathered, axis=1, keepdims=True)) * weight


def diag_kernel(gathered, weight):
    return jnp.broadcast_to(0.75 * weight, gathered.shape)


def first_sums(local_terms, dt_local, reduce_terms):
    return (reduce_terms(local_terms), lax.pmin(dt_local, ("px", "py")))


def norm_only(local_terms):
    return (lax.psum(local_terms[0], ("px", "py")),)


def local(
    displacement,
    velocity,
    external_force,
    lumped_mass,
    thickness,
    added_mass,
    stiffness,
    elements,
    counts,
):
    row_count, col_count = lumped_mass.shape
    stride = col_count + 2
    element_ids = elements.reshape(-1)
    live_count = counts.reshape(())
    active = (jnp.arange(element_ids.shape[0], dtype=jnp.int32) < live_count).astype(jnp.float32)

    def interior(extended):
        return extended.reshape(extended.shape[0], row_count + 2, col_count + 2)[:, 1:-1, 1:-1]

    def stiff_kernel(gathered, weight):
        return (jnp.dot(stiffness, gathered.reshape(24, -1), precision=highest) * weight).reshape(
            gathered.shape
        )

    payload = jnp.concatenate(
        [displacement, thickness[None], added_mass[None], lumped_mass[None]], axis=0
    )
    edged = extended_2(payload, (("px", 1), ("py", 2)), 1).reshape(9, -1)
    disp_edge = edged[:6]
    thick_edge = edged[6]
    added_edge = edged[7]
    mass_edge = edged[8]
    weight_thick = thick_edge[element_ids] * active
    weight_added = added_edge[element_ids] * active
    corners = corner_nodes(element_ids, stride)
    mass_sum = jnp.sum(mass_edge[corners], axis=0)
    stable = 0.5 * jnp.sqrt((added_edge[element_ids] + 0.25 * mass_sum) / thick_edge[element_ids])
    dt_local = jnp.min(jnp.where(active > 0, stable, 1e30))
    internal = interior(assemble(disp_edge, element_ids, weight_thick, stiff_kernel, stride))
    unit_field = jnp.ones((1, mass_edge.shape[0]), jnp.float32)
    precond = lumped_mass[None] + interior(
        assemble(unit_field, element_ids, weight_added, diag_kernel, stride)
    )
    residual = external_force - internal
    acceleration = jnp.zeros_like(residual)
    scaled = residual / precond
    direction = scaled
    (gamma_now,), min_step = first_sums((jnp.sum(residual * scaled),), dt_local, norm_only)
    for sweep in range(ITERS):
        apply_extended = extended_2(direction, (("px", 1), ("py", 2)), 1).reshape(6, -1)
        applied = lumped_mass[None] * direction + interior(
            assemble(apply_extended, element_ids, weight_added, mass_kernel, stride)
        )
        step_length = gamma_now / lax.psum(jnp.sum(direction * applied), ("px", "py"))
        acceleration = acceleration + step_length * direction
        if sweep + 1 < ITERS:
            residual = residual - step_length * applied
            scaled = residual / precond
            (gamma_next,) = norm_only((jnp.sum(residual * scaled),))
            direction = scaled + gamma_next / gamma_now * direction
            gamma_now = gamma_next
    new_velocity = velocity + min_step * acceleration
    new_displacement = displacement + min_step * new_velocity
    return (new_velocity, new_displacement)


def solution(mesh):
    return jax.shard_map(
        local,
        mesh=mesh,
        in_specs=(
            P(None, "px", "py"),
            P(None, "px", "py"),
            P(None, "px", "py"),
            P("px", "py"),
            P("px", "py"),
            P("px", "py"),
            P(),
            P("px", "py"),
            P("px", "py"),
        ),
        out_specs=(P(None, "px", "py"), P(None, "px", "py")),
        check_vma=False,
    )
```

profile of v0, /device:TPU:1, one launch (start us, length us, event | category | flops | bytes accessed | tf_op | source)
XLA Modules:
  0.0 1236.8 jit_solution(369683350031647792)
XLA Ops:
  1.5 4.4 collective-permute-start
  11.3 4.9 collective-permute-start.2
  16.2 3.0 collective-permute-start.3
  19.9 2.0 collective-permute-done.3
  23.0 28.7 %gather_fusion.1 = f32[5120]{0:T(1024)S(1)} fusion(f32[1300]{0:T(1024)S(1)} %squeeze.10, s32[5120]{0:T(1024)S(1)} %broadcast_clamp_fusion), kind=kCustom, calls=%fused_computation.1 | custom fusion | bytes 61440 | tf_op jit(solution)/shard_map/gather | solution.py:88
  51.9 7.1 gather_fusion
  59.0 7.1 gather_fusion.2
  66.4 13.4 %gather_fusion.3 = f32[5120,6]{1,0:T(8,128)S(1)} fusion(f32[6,1300]{0,1:T(8,128)S(1)} %copy.34, s32[5120]{0:T(1024)S(1)} %broadcast_clamp_fusion), kind=kCustom, calls=%fused_computation.3 | custom fusion | bytes 266240 | tf_op jit(solution)/shard_map/gather | solution.py:32
  82.5 28.7 %scatter_custom_fusion = f32[6,1300]{0,1:T(8,128)S(1)} fusion(s32[5120]{0:T(1024)S(1)} %bitcast.95, f32[6,5120]{0,1:T(8,128)S(1)} %copy.36, f32[]{:T(128)} %constant.11.clone.1), kind=kCustom, calls=%fused_computation.26 | custom fusion | flops 30720 | bytes 2652644 | tf_op jit(solution)/shard_map/scatter-add | solution.py:33
  111.6 33.7 %scatter_custom_fusion.1 = f32[1300]{0:T(1024)S(1)} fusion(s32[5120]{0:T(1024)} %bitcast.96, f32[5120]{0:T(1024)S(1)} %reshape.435, f32[]{:T(128)} %constant.11.clone.1), kind=kCustom, calls=%fused_computation.94 | custom fusion | flops 5120 | bytes 5712 | tf_op jit(solution)/shard_map/scatter-add | solution.py:33
  145.6 5.3 collective-permute-start.4
  152.2 3.0 collective-permute-done.5
  155.3 4.3 collective-permute-start.6
  159.5 1.9 collective-permute-start.7
  161.5 3.4 collective-permute-done.7
  165.5 13.4 %gather_fusion.4 = f32[5120,6]{1,0:T(8,128)S(1)} fusion(f32[6,1300]{0,1:T(8,128)S(1)} %copy.38, s32[5120]{0:T(1024)S(1)} %broadcast_clamp_fusion), kind=kCustom, calls=%fused_computation.4 | custom fusion | bytes 266240 | tf_op jit(solution)/shard_map/gather | solution.py:32
  179.4 2.2 bitcast_multiply_fusion.3
  181.6 28.8 %scatter_custom_fusion.2 = f32[6,1300]{0,1:T(8,128)S(1)} fusion(s32[5120]{0:T(1024)} %bitcast.97, f32[6,5120]{0,1:T(8,128)S(1)} %bitcast_multiply_fusion.3, f32[]{:T(128)} %constant.11.clone.1), kind=kCustom, calls=%fused_computation.23 | custom fusion | flops 30720 | bytes 154592 | tf_op jit(solution)/shard_map/scatter-add | solution.py:33
  211.5 111.3 %all-reduce = (f32[]{:T(128)}, f32[]{:T(128)}) all-reduce(f32[]{:T(128)} %get-tuple-element.3, f32[]{:T(128)} %get-tuple-element.2), channel_id=1, replica_groups=mesh['px'=16,'py'=32] {'px','py'}, use_global_device_ids=true, to_apply=%region_6.7 | all-reduce | flops 2 | bytes 16 | tf_op jit(solution)/shard_map/psum | solution.py:49
  324.9 99.4 %psum.58 = f32[]{:T(128)} all-reduce(f32[]{:T(128)} %get-tuple-element.10), channel_id=1, replica_groups=mesh['px'=16,'py'=32] {'px','py'}, use_global_device_ids=true, to_apply=%region_12.13 | all-reduce | flops 1 | bytes 8 | tf_op jit(solution)/shard_map/psum | solution.py:49
  425.6 3.7 collective-permute-start.8
  430.6 3.0 collective-permute-done.9
  433.7 4.7 collective-permute-start.10
  438.4 1.9 collective-permute-start.11
  440.4 3.5 collective-permute-done.11
  444.3 13.4 %gather_fusion.5 = f32[5120,6]{1,0:T(8,128)S(1)} fusion(f32[6,1300]{0,1:T(8,128)S(1)} %copy.40, s32[5120]{0:T(1024)S(1)} %broadcast_clamp_fusion), kind=kCustom, calls=%fused_computation.5 | custom fusion | bytes 266240 | tf_op jit(solution)/shard_map/gather | solution.py:32
  458.3 2.2 bitcast_multiply_fusion.2
  460.5 28.8 %scatter_custom_fusion.3 = f32[6,1300]{0,1:T(8,128)S(1)} fusion(s32[5120]{0:T(1024)} %bitcast.98, f32[6,5120]{0,1:T(8,128)S(1)} %bitcast_multiply_fusion.2, f32[]{:T(128)} %constant.11.clone.1), kind=kCustom, calls=%fused_computation.20 | custom fusion | flops 30720 | bytes 154592 | tf_op jit(solution)/shard_map/scatter-add | solution.py:33
  490.4 103.0 %psum.59 = f32[]{:T(128)} all-reduce(f32[]{:T(128)} %multiply_reduce_fusion.3), channel_id=1, replica_groups=mesh['px'=16,'py'=32] {'px','py'}, use_global_device_ids=true, to_apply=%region_16.17 | all-reduce | flops 1 | bytes 8 | tf_op jit(solution)/shard_map/psum | solution.py:106
  595.3 99.6 %psum.60 = f32[]{:T(128)} all-reduce(f32[]{:T(128)} %get-tuple-element.8), channel_id=1, replica_groups=mesh['px'=16,'py'=32] {'px','py'}, use_global_device_ids=true, to_apply=%region_18.19 | all-reduce | flops 1 | bytes 8 | tf_op jit(solution)/shard_map/psum | solution.py:49
  696.2 3.7 collective-permute-start.12
  701.2 3.0 collective-permute-done.13
  704.3 4.9 collective-permute-start.14
  711.2 3.5 collective-permute-done.15
  715.1 13.4 %gather_fusion.6 = f32[5120,6]{1,0:T(8,128)S(1)} fusion(f32[6,1300]{0,1:T(8,128)S(1)} %copy.42, s32[5120]{0:T(1024)S(1)} %broadcast_clamp_fusion), kind=kCustom, calls=%fused_computation.6 | custom fusion | bytes 266240 | tf_op jit(solution)/shard_map/gather | solution.py:32
  729.1 2.2 bitcast_multiply_fusion.1
  731.3 29.0 %scatter_custom_fusion.4 = f32[6,1300]{0,1:T(8,128)S(1)} fusion(s32[5120]{0:T(1024)} %bitcast.99, f32[6,5120]{0,1:T(8,128)S(1)} %bitcast_multiply_fusion.1, f32[]{:T(128)} %constant.11.clone.1), kind=kCustom, calls=%fused_computation.17 | custom fusion | flops 30720 | bytes 154592 | tf_op jit(solution)/shard_map/scatter-add | solution.py:33
  761.4 102.6 %psum.61 = f32[]{:T(128)} all-reduce(f32[]{:T(128)} %multiply_reduce_fusion.1), channel_id=1, replica_groups=mesh['px'=16,'py'=32] {'px','py'}, use_global_device_ids=true, to_apply=%region_22.23 | all-reduce | flops 1 | bytes 8 | tf_op jit(solution)/shard_map/psum | solution.py:106
  866.0 99.5 %psum.62 = f32[]{:T(128)} all-reduce(f32[]{:T(128)} %multiply_reduce_fusion), channel_id=1, replica_groups=mesh['px'=16,'py'=32] {'px','py'}, use_global_device_ids=true, to_apply=%region_24.25 | all-reduce | flops 1 | bytes 8 | tf_op jit(solution)/shard_map/psum | solution.py:49
  967.0 3.7 collective-permute-start.16
  972.0 3.0 collective-permute-done.17
  975.1 4.9 collective-permute-start.18
  982.0 3.5 collective-permute-done.19
  985.9 13.4 %gather_fusion.7 = f32[5120,6]{1,0:T(8,128)S(1)} fusion(f32[6,1300]{0,1:T(8,128)S(1)} %copy.44, s32[5120]{0:T(1024)S(1)} %broadcast_clamp_fusion), kind=kCustom, calls=%fused_computation.7 | custom fusion | bytes 266240 | tf_op jit(solution)/shard_map/gather | solution.py:32
  999.9 2.2 bitcast_multiply_fusion
  1002.1 28.8 %scatter_custom_fusion.5 = f32[6,1300]{0,1:T(8,128)S(1)} fusion(s32[5120]{0:T(1024)} %bitcast.100, f32[6,5120]{0,1:T(8,128)S(1)} %bitcast_multiply_fusion, f32[]{:T(128)} %constant.11.clone.1), kind=kCustom, calls=%fused_computation.14 | custom fusion | flops 30720 | bytes 154592 | tf_op jit(solution)/shard_map/scatter-add | solution.py:33
  1032.0 102.7 %pmin.7 = f32[]{:T(128)} all-reduce(f32[]{:T(128)} %get-tuple-element.40), channel_id=1, replica_groups=mesh['px'=16,'py'=32] {'px','py'}, use_global_device_ids=true, to_apply=%region_2.3 | all-reduce | flops 1 | bytes 8 | tf_op jit(solution)/shard_map/pmin | solution.py:45
  1134.7 99.5 %psum.63 = f32[]{:T(128)} all-reduce(f32[]{:T(128)} %fusion.17), channel_id=1, replica_groups=mesh['px'=16,'py'=32] {'px','py'}, use_global_device_ids=true, to_apply=%region_28.29 | all-reduce | flops 1 | bytes 8 | tf_op jit(solution)/shard_map/psum | solution.py:106
  (126 shorter events, 32.1 us)
Async XLA Ops:
  0.6 80.8 %copy-start = (f32[24,24]{1,0:T(8,128)S(1)}, f32[24,24]{1,0:T(8,128)}, u32[]{:S(2)}) copy-start(f32[24,24]{1,0:T(8,128)} %param.15) | copy-start | bytes 6916
  1.5 8.0 collective-permute-start
  5.9 4.5 collective-permute-start.1
  8.8 73.8 %copy-start.6 = (s32[5120,1]{0,1:T(1,128)}, s32[5120,1]{0,1:T(1,128)S(1)}, u32[]{:S(2)}) copy-start(s32[5120,1]{0,1:T(1,128)S(1)} %compare_select_fusion) | copy-start | bytes 61444
  11.3 8.6 collective-permute-start.2
  16.2 5.7 collective-permute-start.3
  22.9 28.8 %copy-start.1 = (f32[9,10,130]{2,1,0:T(8,128)}, f32[9,10,130]{2,1,0:T(8,128)S(1)}, u32[]{:S(2)}) copy-start(f32[9,10,130]{2,1,0:T(8,128)S(1)} %pad_maximum_fusion) | copy-start | bytes 140404
  59.0 7.1 slice-start
  82.5 62.9 %copy-start.2 = (f32[8,128]{1,0:T(8,128)S(1)}, f32[8,128]{1,0:T(8,128)}, u32[]{:S(2)}) copy-start(f32[8,128]{1,0:T(8,128)} %param.12) | copy-start | bytes 12292
  82.5 63.0 %copy-start.4 = (f32[6,8,128]{2,1,0:T(8,128)S(1)}, f32[6,8,128]{2,1,0:T(8,128)}, u32[]{:S(2)}) copy-start(f32[6,8,128]{2,1,0:T(8,128)} %param.11) | copy-start | bytes 73732
  145.6 6.6 collective-permute-start.4
  150.8 4.3 collective-permute-start.5
  155.3 6.2 collective-permute-start.6
  159.5 5.4 collective-permute-start.7
  425.6 5.0 collective-permute-start.8
  429.3 4.3 collective-permute-start.9
  433.7 6.7 collective-permute-start.10
  438.4 5.4 collective-permute-start.11
  696.2 5.0 collective-permute-start.12
  699.9 4.3 collective-permute-start.13
  704.3 6.8 collective-permute-start.14
  709.2 5.4 collective-permute-start.15
  967.0 5.0 collective-permute-start.16
  970.7 4.3 collective-permute-start.17
  975.1 6.8 collective-permute-start.18
  980.0 5.4 collective-permute-start.19
  1002.1 233.4 %copy-start.3 = (f32[6,8,128]{2,1,0:T(8,128)S(1)}, f32[6,8,128]{2,1,0:T(8,128)}, u32[]{:S(2)}) copy-start(f32[6,8,128]{2,1,0:T(8,128)} %param.9) | copy-start | bytes 73732
  1002.1 233.4 %copy-start.5 = (f32[6,8,128]{2,1,0:T(8,128)S(1)}, f32[6,8,128]{2,1,0:T(8,128)}, u32[]{:S(2)}) copy-start(f32[6,8,128]{2,1,0:T(8,128)} %param.10) | copy-start | bytes 73732
where the time goes:
time: 1240 us
  blocking collectives  818 us (66%)
  other arithmetic  200 us (16%)
  local copies, waits for them, and re-layouts  117 us (9%)
  starting transfers between devices  61.5 us (5%)
  waiting for transfers between devices  28.9 us (2%)
    psum x4, blocking collectives, norm_only(): return (lax.psum(local_terms[0], ('px', 'py')),)  410 us
    psum x3, blocking collectives, local(): lax.psum(jnp.sum(direction * applied), ('px', 'py'))  305 us
    scatter-add x6, other arithmetic, assemble(): summed.at[:, corners.reshape(-1)].add(values.reshape(extended.shape[0], -1))  178 us
    pmin x1, blocking collectives, first_sums(): return (reduce_terms(local_terms), lax.pmin(dt_local, ('px', 'py')))  103 us
    gather x6, local copies, waits for them, and re-layouts, assemble(): values = kernel(extended[:, corners], weight)  67.9 us
    ppermute x10, starting transfers between devices, extended_2(): before = lax.ppermute(last, axis, up)  44.3 us
    ppermute x10, waiting for transfers between devices, extended_2(): after = lax.ppermute(first, axis, down)  28.9 us
    gather x2, local copies, waits for them, and re-layouts, local(): mass_sum = jnp.sum(mass_edge[corners], axis=0)  28.7 us
  transfers between devices with their start and end apart: 20, of which 10 were waited for; matrix products, arithmetic and copies ran while one was open for 0% of the time, Pallas kernels for 0%

commit v1 on v0

v1 whole, which is shorter than its diff:
```python
import functools

import jax
import jax.numpy as jnp
from jax import lax
from jax.experimental import pallas as pl
from jax.experimental.pallas import tpu as pltpu
from jax.sharding import PartitionSpec as P

ITERS = 4
MESH = pl.DeviceIdType.MESH
WIDE = 5
F32 = jnp.float32
BF16 = jnp.bfloat16


def quadratic(left, right, moments):
    total = None
    for i, a in enumerate(left):
        inner = None
        for j, b in enumerate(right):
            term = b * moments[i + j]
            inner = term if inner is None else inner + term
        total = a * inner if total is None else total + a * inner
    return total


def coefficients(mu):
    one = jnp.ones_like(mu[0])
    zero = jnp.zeros_like(mu[0])
    energy = [mu[k] - mu[k + 1] for k in range(7)]
    scaled, direction = [one], [one]
    gamma = mu[0]
    accel = [zero] * ITERS
    for sweep in range(ITERS):
        curvature = quadratic(direction, direction, energy)
        step = jnp.clip(gamma / curvature, 0.74, 26.0)
        for i, d in enumerate(direction):
            accel[i] = accel[i] + step * d
        if sweep + 1 < ITERS:
            applied = direction + [zero]
            for i, d in enumerate(direction):
                applied[i + 1] = applied[i + 1] - d
            grown = scaled + [zero]
            scaled = [s - step * a for s, a in zip(grown, applied)]
            gamma_next = jnp.maximum(quadratic(scaled, scaled, mu), 0.0)
            ratio = gamma_next / gamma
            direction = [s + ratio * d for s, d in zip(scaled, direction + [zero])]
            gamma = gamma_next
    return accel


def kernel(
    n_px,
    n_py,
    disp,
    vel,
    force,
    mass,
    thick,
    added,
    stiff,
    elements,
    counts,
    out_vel,
    out_disp,
    own,
    weights,
    vel_v,
    stiff_v,
    elem_v,
    count_v,
    above,
    below,
    strip_out,
    strip_left,
    strip_right,
    row_plane,
    row_line,
    got_plane,
    got_line,
    in_sem,
    halo_send,
    halo_recv,
    red_send,
    red_recv,
):
    px = lax.axis_index("px")
    py = lax.axis_index("py")
    up, down = lax.rem(px + n_px - 1, n_px), lax.rem(px + 1, n_px)
    left, right = lax.rem(py + n_py - 1, n_py), lax.rem(py + 1, n_py)

    barrier = pltpu.get_barrier_semaphore()

    def greet(a, b):
        pl.semaphore_signal(barrier, inc=1, device_id=(a, b), device_id_type=MESH)

    for a in (up, down):
        for b in (left, right):
            greet(a, b)
    for k in range(1, n_py):
        greet(px, lax.rem(py + k, n_py))
    for k in range(1, n_px):
        greet(lax.rem(px + k, n_px), py)

    loads = [
        pltpu.make_async_copy(src, dst, in_sem.at[i])
        for i, (src, dst) in enumerate(
            (
                (elements, elem_v),
                (counts, count_v),
                (thick, weights.at[0]),
                (added, weights.at[1]),
                (stiff, stiff_v),
                (disp, own.at[0:6]),
                (force, own.at[6:12]),
                (mass, own.at[12]),
                (vel, vel_v),
            )
        )
    ]
    for load in loads:
        load.start()

    row8 = lax.broadcasted_iota(jnp.int32, (8, 128), 0)
    lane8 = lax.broadcasted_iota(jnp.int32, (8, 128), 1)

    loads[0].wait()
    loads[1].wait()
    ids = elem_v[...]
    tiles = ids.shape[0]
    slot = lax.broadcasted_iota(jnp.int32, (tiles, 128), 0) * 128 + lax.broadcasted_iota(
        jnp.int32, (tiles, 128), 1
    )
    id_row = lax.shift_right_logical(ids * 4033, 19)
    id_col = ids - id_row * 130
    id_row = jnp.where(slot < count_v[...], id_row, -1)
    row_sel = lax.broadcasted_iota(jnp.int32, (8, 128), 0) + 1
    col_sel = lax.broadcasted_iota(jnp.int32, (128, 128), 0) + 1
    hot_rows, hot_cols = [], []
    for t in range(tiles):
        hot_rows.append(
            jnp.where(jnp.broadcast_to(id_row[t : t + 1], (8, 128)) == row_sel, 1.0, 0.0).astype(BF16)
        )
        hot_cols.append(
            jnp.where(jnp.broadcast_to(id_col[t : t + 1], (128, 128)) == col_sel, 1.0, 0.0).astype(BF16)
        )
    live = lax.dot_general(
        jnp.concatenate(hot_rows, axis=1),
        jnp.concatenate(hot_cols, axis=1),
        (((1,), (1,)), ((), ())),
        preferred_element_type=F32,
    )
    loads[2].wait()
    loads[3].wait()
    own[13] = weights[0] * live
    own[14] = weights[1] * live

    for i in (5, 6, 7):
        loads[i].wait()
    pack_right = jnp.zeros((8, 128), F32)
    pack_left = jnp.zeros((8, 128), F32)
    group = lax.shift_right_logical(lane8, 3)
    for f in range(15):
        field = own[f]
        pack_right = jnp.where(group == f, pltpu.roll(field, (8 * f + 8) % 128, 1), pack_right)
        pack_left = jnp.where(group == f, pltpu.roll(field, 8 * f, 1), pack_left)
    strip_out[0] = pack_right
    strip_out[1] = pack_left

    loads[4].wait()
    spread = jnp.where(
        lax.shift_right_logical(lax.broadcasted_iota(jnp.int32, (192, 24), 0), 3)
        == lax.broadcasted_iota(jnp.int32, (192, 24), 1),
        1.0,
        0.0,
    ).astype(BF16)
    same_row = (lax.broadcasted_iota(jnp.int32, (192, 192), 0) & 7) == (
        lax.broadcasted_iota(jnp.int32, (192, 192), 1) & 7
    )

    def expand(part):
        tall = jnp.dot(spread, part, preferred_element_type=F32).astype(BF16)
        full = lax.dot_general(tall, spread, (((1,), (1,)), ((), ())), preferred_element_type=F32)
        return jnp.where(same_row, full, 0.0).astype(BF16)

    stiff_all = stiff_v[...]
    stiff_hi = stiff_all.astype(BF16)
    stiff_lo = (stiff_all - stiff_hi.astype(F32)).astype(BF16)
    big_hi, big_lo = expand(stiff_hi), expand(stiff_lo)

    pl.semaphore_wait(barrier, 4 + (n_py - 1) + (n_px - 1))

    plan = (
        (own.at[:, 8 - WIDE : 8, :], above.at[:, 8 - WIDE : 8, :], down, py),
        (own.at[:, 0:WIDE, :], below.at[:, 0:WIDE, :], up, py),
        (strip_out.at[0], strip_left.at[1], px, right),
        (strip_out.at[1], strip_right.at[1], px, left),
        (strip_out.at[0], strip_left.at[0], down, right),
        (strip_out.at[1], strip_right.at[0], down, left),
        (strip_out.at[0], strip_left.at[2], up, right),
        (strip_out.at[1], strip_right.at[2], up, left),
    )
    halo = [
        pltpu.make_async_remote_copy(
            src_ref=src,
            dst_ref=dst,
            send_sem=halo_send.at[i],
            recv_sem=halo_recv.at[i],
            device_id=(a, b),
            device_id_type=MESH,
        )
        for i, (src, dst, a, b) in enumerate(plan)
    ]
    for copy in halo:
        copy.start()
    for copy in halo:
        copy.wait()

    def extend(f):
        out = []
        for i in range(3):
            if i == 0:
                main = jnp.where(row8 >= 8 - WIDE, above[f], 0.0)
            elif i == 1:
                main = own[f]
            else:
                main = jnp.where(row8 < WIDE, below[f], 0.0)
            side = jnp.where(
                lane8 >= 128 - WIDE,
                pltpu.roll(strip_left[i], (120 - 8 * f) % 128, 1),
                jnp.where(lane8 < WIDE, pltpu.roll(strip_right[i], (128 - 8 * f) % 128, 1), 0.0),
            )
            out.append(jnp.concatenate([main, side], axis=1))
        return jnp.concatenate(out, axis=0)

    def next_col(x):
        return pltpu.roll(x, x.shape[1] - 1, 1)

    def prev_col(x):
        return pltpu.roll(x, 1, 1)

    def next_row(x):
        return pltpu.roll(x, x.shape[0] - 1, 0)

    def prev_row(x):
        return pltpu.roll(x, 1, 0)

    def four_sum(x):
        half = x + next_col(x)
        return half + next_row(half)

    def to_nodes(x):
        half = x + prev_row(x)
        return half + prev_col(half)

    def six(x):
        return jnp.concatenate([x] * 6, axis=0)

    field_mass, field_thick, field_added = extend(12), extend(13), extend(14)
    weight_sum = to_nodes(field_added)
    precond = field_mass + 0.75 * weight_sum
    inverse = 1.0 / precond
    quarter = 0.25 * inverse
    quarter_weight = six(quarter * weight_sum)
    quarter6 = six(quarter)
    added6 = six(field_added)

    u00 = jnp.concatenate([extend(c) for c in range(6)], axis=0)
    u01 = next_col(u00)
    u10 = next_row(u00)
    u11 = next_row(u01)
    corners = (u00, u01, u10, u11)
    forces = [[], [], [], []]
    products = []
    for t in range(3):
        stacked = jnp.concatenate(
            [corners[n][24 * c + 8 * t : 24 * c + 8 * t + 8] for c in range(6) for n in range(4)],
            axis=0,
        )
        hi = stacked.astype(BF16)
        lo = (stacked - hi.astype(F32)).astype(BF16)
        product = (
            jnp.dot(big_hi, lo, preferred_element_type=F32)
            + jnp.dot(big_lo, hi, preferred_element_type=F32)
        ) + jnp.dot(big_hi, hi, preferred_element_type=F32)
        products.append(product)
    for n in range(4):
        forces[n] = jnp.concatenate(
            [
                products[t][8 * (4 * c + n) : 8 * (4 * c + n) + 8] * field_thick[8 * t : 8 * t + 8]
                for c in range(6)
                for t in range(3)
            ],
            axis=0,
        )
    internal = (forces[0] + prev_row(forces[2])) + prev_col(forces[1] + prev_row(forces[3]))
    external = jnp.concatenate([extend(6 + c) for c in range(6)], axis=0)
    powers = [(external - internal) * six(inverse)]
    for k in range(4):
        p = powers[-1]
        powers.append(quarter6 * to_nodes(added6 * four_sum(p)) - quarter_weight * p)

    def own_part(x):
        return [x[24 * c + 8 : 24 * c + 16, 0:128] for c in range(6)]

    mine = [own_part(x) for x in powers]
    mass_own = precond[8:16, 0:128]
    rows = []
    for k in range(8):
        a, b = mine[k // 2], mine[k - k // 2]
        total = a[0] * b[0]
        for c in range(1, 6):
            total = total + a[c] * b[c]
        rows.append(jnp.sum(total * mass_own, axis=0, keepdims=True))
    sums = jnp.sum(jnp.concatenate(rows, axis=0), axis=1, keepdims=True)
    row = jnp.sum(jnp.where(row8 == lane8, sums, 0.0), axis=0, keepdims=True)
    thick_own = own[13]
    around = four_sum(field_mass)[8:16, 0:128]
    stable = 0.5 * jnp.sqrt((weights[1] + 0.25 * around) / weights[0])
    smallest = jnp.min(jnp.where(live > 0, stable, 1e30), keepdims=True)
    lane1 = lax.broadcasted_iota(jnp.int32, (1, 128), 1)
    row = jnp.where(lane1 == 8, smallest, row)

    def gather(row, size, here, src, slots, device, i):
        src[...] = row
        slots[pl.ds(here, 1)] = row.reshape(1, 1, 128)
        for k in range(1, size):
            there = lax.rem(here + k, size)
            pltpu.make_async_remote_copy(
                src_ref=src,
                dst_ref=slots.at[here],
                send_sem=red_send.at[i],
                recv_sem=red_recv.at[i],
                device_id=device(there),
                device_id_type=MESH,
            ).start()
        most = slots.at[pl.ds(0, size - 1)]
        pltpu.make_async_copy(most, most, red_recv.at[i]).wait()
        pltpu.make_async_copy(most, most, red_send.at[i]).wait()
        sums = [slots[k] for k in range(size)]
        lows = sums
        while len(sums) > 1:
            odd = len(sums) % 2
            sums, lows = (
                [sums[j] + sums[j + 1] for j in range(0, len(sums) - odd, 2)] + sums[len(sums) - odd :],
                [jnp.minimum(lows[j], lows[j + 1]) for j in range(0, len(lows) - odd, 2)]
                + lows[len(lows) - odd :],
            )
        return jnp.where(lane1 == 8, lows[0], sums[0])

    row = gather(row, n_py, py, row_plane, got_plane, lambda there: (px, there), 0)
    row = gather(row, n_px, px, row_line, got_line, lambda there: (there, py), 1)

    accel = coefficients([row[:, k : k + 1] for k in range(8)])
    min_step = row[:, 8:9]
    loads[8].wait()
    for c in range(6):
        total = accel[0] * mine[0][c]
        for k in range(1, ITERS):
            total = total + accel[k] * mine[k][c]
        new_vel = vel_v[c] + min_step * total
        out_vel[c] = new_vel
        out_disp[c] = own[c] + min_step * new_vel


def local(n_px, n_py, *args):
    shape = args[0].shape
    tiles = args[7].shape[0]
    vmem = lambda *dims: pltpu.VMEM(dims, F32)
    return tuple(
        pl.pallas_call(
            functools.partial(kernel, n_px, n_py),
            out_shape=[jax.ShapeDtypeStruct(shape, F32)] * 2,
            in_specs=[pl.BlockSpec(memory_space=pl.ANY)] * 9,
            out_specs=[pl.BlockSpec(memory_space=pltpu.VMEM)] * 2,
            scratch_shapes=[
                vmem(15, 8, 128),
                vmem(2, 8, 128),
                vmem(6, 8, 128),
                vmem(24, 24),
                pltpu.VMEM((tiles, 128), jnp.int32),
                pltpu.VMEM((1, 1), jnp.int32),
                vmem(15, 8, 128),
                vmem(15, 8, 128),
                vmem(2, 8, 128),
                vmem(3, 8, 128),
                vmem(3, 8, 128),
                vmem(1, 128),
                vmem(1, 128),
                vmem(n_py, 1, 128),
                vmem(n_px, 1, 128),
                pltpu.SemaphoreType.DMA((9,)),
                pltpu.SemaphoreType.DMA((8,)),
                pltpu.SemaphoreType.DMA((8,)),
                pltpu.SemaphoreType.DMA((2,)),
                pltpu.SemaphoreType.DMA((2,)),
            ],
            compiler_params=pltpu.CompilerParams(collective_id=0, has_side_effects=True),
            name="crash_step",
        )(*args)
    )


def solution(mesh):
    field = P(None, "px", "py")
    plane = P("px", "py")
    return jax.shard_map(
        functools.partial(local, mesh.shape["px"], mesh.shape["py"]),
        mesh=mesh,
        in_specs=(field, field, field, plane, plane, plane, P(), plane, plane),
        out_specs=(field, field),
        check_vma=False,
    )
```

time: 1240 us -> 38 us (0.03)
  blocking collectives: 818 us -> 0 us
  other arithmetic: 200 us -> 0 us
  local copies, waits for them, and re-layouts: 117 us -> 1.96 us
  starting transfers between devices: 61.5 us -> 0 us
  Pallas kernels: 0 us -> 34.5 us
  waiting for transfers between devices: 28.9 us -> 0 us
    psum x7 -> x0, blocking collectives: 715 us -> none  [the longest x4 410 us: norm_only(): return (lax.psum(local_terms[0], ('px', 'py')),)]
    scatter-add x6 -> x0, other arithmetic: 178 us -> none  [assemble(): summed.at[:, corners.reshape(-1)].add(values.reshape(extended.shape[0], -1))]
    gather x10 -> x0, local copies, waits for them, and re-layouts: 111 us -> none  [the longest x6 67.9 us: assemble(): values = kernel(extended[:, corners], weight)]
    pmin x1 -> x0, blocking collectives: 103 us -> none  [first_sums(): return (reduce_terms(local_terms), lax.pmin(dt_local, ('px', 'py')))]
    ppermute x20 -> x0, starting transfers between devices: 61.5 us -> none  [the longest x10 44.3 us: extended_2(): before = lax.ppermute(last, axis, up)]
    pallas_call x0 -> x1, Pallas kernels: none -> 34.5 us  [local(): pl.pallas_call(functools.partial(kernel, n_px, n_py), out_shape=[jax.Shap...]
    ppermute x20 -> x0, waiting for transfers between devices: 28.9 us -> none  [the longest x10 28.9 us: extended_2(): after = lax.ppermute(first, axis, down)]
  transfers between devices with their start and end apart: 20 -> 0, of which waited for: 10 -> 0; matrix products, arithmetic and copies ran while one was open for 0% -> 0% of each run, Pallas kernels for 0% -> 0%
where the time goes in v1:
time: 38 us; the launch traced here: 37.8 us
  Pallas kernels  34.5 us (91%)
  local copies, waits for them, and re-layouts  1.96 us (5%)
  between operations  1.3 us (3%)
    pallas_call x1, Pallas kernels, local(): pl.pallas_call(functools.partial(kernel, n_px, n_py), out_shape=[jax.Shap...  34.5 us
    unnamed x4, local copies, waits for them, and re-layouts  1.96 us

profile of v1, /device:TPU:1, one launch (start us, length us, event | category | flops | bytes accessed | tf_op | source)
XLA Modules:
  0.0 37.8 jit_solution(1976328274783393958)
XLA Ops:
  1.3 34.5 %crash_step.1 = (f32[6,8,128]{2,1,0:T(8,128)}, f32[6,8,128]{2,1,0:T(8,128)}) custom-call(f32[6,8,128]{2,1,0:T(8,128)} %disp.1, f32[6,8,128]{2,1,0:T(8,128)} %vel.1, f32[6,8,128]{2,1,0:T(8,128)} %force.1, f32[8,128]{1,0:T(8,128)} %mass.1, f32[8,128]{1,0:T(8,128)} %thick.1, f32[8,128]{1,0:T(8,128)} %added.1, f32[24,24]{1,0:T(8,128)} %stiff.1, ...), custom_call_target="tpu_custom_call" | custom-call | tf_op jit(solution)/shard_map/crash_step/pallas_call | solution.py:372
  35.8 0.0 copy-start
  35.8 1.4 %copy.14 = f32[6,8,128]{2,1,0:T(8,128)} copy(f32[6,8,128]{2,1,0:T(8,128)} %get-tuple-element.4) | data formatting | bytes 49152
  37.2 0.0 copy-done
  37.2 0.6 %copy.15 = f32[6,8,128]{2,1,0:T(8,128)} copy(f32[6,8,128]{2,1,0:T(8,128)S(1)} %copy-done) | data formatting | bytes 49152
Async XLA Ops:
  35.8 1.4 %copy-start = (f32[6,8,128]{2,1,0:T(8,128)S(1)}, f32[6,8,128]{2,1,0:T(8,128)}, u32[]{:S(2)}) copy-start(f32[6,8,128]{2,1,0:T(8,128)} %get-tuple-element.5) | copy-start | bytes 73732

commit v2 on v1

v2 whole, which is shorter than its diff:
```python
import functools

import jax
import jax.numpy as jnp
from jax import lax
from jax.experimental import pallas as pl
from jax.experimental.pallas import tpu as pltpu
from jax.sharding import PartitionSpec as P

ITERS = 4
FIELDS = 15
MESH = pl.DeviceIdType.MESH
F32 = jnp.float32
BF16 = jnp.bfloat16


def quadratic(left, right, moments):
    total = None
    for i, a in enumerate(left):
        inner = None
        for j, b in enumerate(right):
            term = b * moments[i + j]
            inner = term if inner is None else inner + term
        total = a * inner if total is None else total + a * inner
    return total


def coefficients(mu):
    one = jnp.ones_like(mu[0])
    zero = jnp.zeros_like(mu[0])
    energy = [mu[k] - mu[k + 1] for k in range(7)]
    scaled, direction = [one], [one]
    gamma = mu[0]
    accel = [zero] * ITERS
    for sweep in range(ITERS):
        curvature = quadratic(direction, direction, energy)
        step = jnp.clip(gamma / curvature, 0.74, 26.0)
        for i, d in enumerate(direction):
            accel[i] = accel[i] + step * d
        if sweep + 1 < ITERS:
            applied = direction + [zero]
            for i, d in enumerate(direction):
                applied[i + 1] = applied[i + 1] - d
            scaled = [s - step * a for s, a in zip(scaled + [zero], applied)]
            gamma_next = jnp.maximum(quadratic(scaled, scaled, mu), 0.0)
            ratio = gamma_next / gamma
            direction = [s + ratio * d for s, d in zip(scaled, direction + [zero])]
            gamma = gamma_next
    return accel


def base_of(f):
    return 9 * f + 4 if f < 6 else 54 + 8 * (f - 6) + 4


def kernel(
    n_px,
    n_py,
    disp,
    force,
    mass,
    thick,
    added,
    stiff,
    elements,
    counts,
    out_gain,
    out_step,
    own,
    weights,
    stiff_v,
    elem_v,
    count_v,
    above,
    below,
    strip_out,
    strips,
    row_plane,
    row_line,
    got_plane,
    got_line,
    in_sem,
    halo_send,
    halo_recv,
    red_send,
    red_recv,
    relay,
):
    px = lax.axis_index("px")
    py = lax.axis_index("py")

    def at_px(k):
        return lax.rem(px + (n_px + k), n_px)

    def at_py(k):
        return lax.rem(py + (n_py + k), n_py)

    loads = [
        pltpu.make_async_copy(src, dst, in_sem.at[i])
        for src, dst, i in (
            (elements, elem_v, 0),
            (counts, count_v, 1),
            (thick, weights.at[0], 2),
            (added, weights.at[1], 2),
            (disp, own.at[0:6], 3),
            (force, own.at[6:12], 3),
            (mass, own.at[12], 3),
            (stiff, stiff_v, 4),
        )
    ]
    for load in loads:
        load.start()

    up, down, left, right = at_px(-1), at_px(1), at_py(-1), at_py(1)
    barrier = pltpu.get_barrier_semaphore()

    def signal(sem, a, b):
        pl.semaphore_signal(sem, inc=1, device_id=(a, b), device_id_type=MESH)

    around = [(up, left), (up, py), (up, right), (px, left), (px, right), (down, left), (down, py), (down, right)]
    for a, b in around:
        signal(barrier, a, b)

    row8 = lax.broadcasted_iota(jnp.int32, (8, 128), 0)
    lane8 = lax.broadcasted_iota(jnp.int32, (8, 128), 1)

    loads[0].wait()
    loads[1].wait()
    ids = elem_v[...]
    tiles = ids.shape[0]
    slot = lax.broadcasted_iota(jnp.int32, (tiles, 128), 0) * 128 + lax.broadcasted_iota(
        jnp.int32, (tiles, 128), 1
    )
    id_row = lax.shift_right_logical(ids * 4033, 19)
    id_col = ids - id_row * 130
    id_row = jnp.where(slot < count_v[...], id_row, -1)
    row_sel = row8 + 1
    col_sel = lax.broadcasted_iota(jnp.int32, (128, 128), 0) + 1
    hot_rows, hot_cols = [], []
    for t in range(tiles):
        hot_rows.append(
            jnp.where(jnp.broadcast_to(id_row[t : t + 1], (8, 128)) == row_sel, 1.0, 0.0).astype(BF16)
        )
        hot_cols.append(
            jnp.where(jnp.broadcast_to(id_col[t : t + 1], (128, 128)) == col_sel, 1.0, 0.0).astype(BF16)
        )
    live = lax.dot_general(
        jnp.concatenate(hot_rows, axis=1),
        jnp.concatenate(hot_cols, axis=1),
        (((1,), (1,)), ((), ())),
        preferred_element_type=F32,
    )
    pltpu.make_async_copy(weights, weights, in_sem.at[2]).wait()
    own[13] = weights[0] * live
    own[14] = weights[1] * live

    pltpu.make_async_copy(own.at[0:13], own.at[0:13], in_sem.at[3]).wait()
    lane_group = jnp.where(
        lane8 < 54, lax.shift_right_logical(lane8 * 57, 9), lax.shift_right_logical(lane8 - 54, 3) + 6
    )
    from_left = jnp.where(lane8 < 54, lane8 - 9 * lane_group, (lane8 - 54) & 7) < 4
    packed = jnp.zeros((8, 128), F32)
    for f in range(FIELDS):
        packed = jnp.where(lane_group == f, pltpu.roll(own[f], base_of(f), 1), packed)
    strip_out[...] = packed

    pl.semaphore_wait(barrier, 8)

    halo = [
        pltpu.make_async_remote_copy(
            src_ref=src,
            dst_ref=dst,
            send_sem=halo_send.at[i],
            recv_sem=halo_recv.at[i],
            device_id=(a, b),
            device_id_type=MESH,
        )
        for src, dst, a, b, i in (
            (strip_out, strips.at[2], down, right, 0),
            (strip_out, strips.at[3], down, left, 0),
            (strip_out, strips.at[4], up, right, 0),
            (strip_out, strips.at[5], up, left, 0),
            (strip_out, strips.at[0], px, right, 0),
            (strip_out, strips.at[1], px, left, 0),
            (own.at[:, 4:8, :], above.at[:, 4:8, :], down, py, 1),
            (own.at[:, 0:5, :], below.at[:, 0:5, :], up, py, 2),
        )
    ]
    for copy in halo:
        copy.start()

    def tell(k, axes):
        far = 1 << k
        if "px" in axes:
            signal(relay.at[k], at_px(far), py)
            signal(relay.at[k], at_px(-far), py)
        if "py" in axes:
            signal(relay.at[k], px, at_py(far))
            signal(relay.at[k], px, at_py(-far))

    rounds = []
    far = 1
    while 2 * far <= max(n_px, n_py) // 2:
        rounds.append([n for n, size in (("px", n_px), ("py", n_py)) if 2 * far <= size // 2])
        far *= 2

    def listen(k):
        pl.semaphore_wait(relay.at[k], 2 * len(rounds[k]))

    def relay_step(k):
        if 1 <= k <= len(rounds):
            listen(k - 1)
        if k < len(rounds):
            tell(k, rounds[k])

    relay_step(0)

    loads[7].wait()
    spread = jnp.where(
        lax.shift_right_logical(lax.broadcasted_iota(jnp.int32, (192, 24), 0), 3)
        == lax.broadcasted_iota(jnp.int32, (192, 24), 1),
        1.0,
        0.0,
    ).astype(BF16)
    same_row = (lax.broadcasted_iota(jnp.int32, (192, 192), 0) & 7) == (
        lax.broadcasted_iota(jnp.int32, (192, 192), 1) & 7
    )

    def expand(part):
        tall = jnp.dot(spread, part, preferred_element_type=F32).astype(BF16)
        full = lax.dot_general(tall, spread, (((1,), (1,)), ((), ())), preferred_element_type=F32)
        return jnp.where(same_row, full, 0.0).astype(BF16)

    stiff_all = stiff_v[...]
    stiff_hi = stiff_all.astype(BF16)
    stiff_lo = (stiff_all - stiff_hi.astype(F32)).astype(BF16)
    big_hi, big_lo = expand(stiff_hi), expand(stiff_lo)

    relay_step(1)
    relay_step(2)

    pltpu.make_async_copy(strips, strips, halo_recv.at[0]).wait()
    halo[6].wait_recv()
    halo[7].wait_recv()

    lower = row8 < 4
    side_mid = jnp.where(from_left, strips[0], strips[1])
    side_above = jnp.where(from_left, strips[2], strips[3])
    side_below = jnp.where(from_left, strips[4], strips[5])
    side_edge = jnp.where(lower, side_below, side_above)
    side_next = pltpu.roll(side_below, 7, 0)

    def unpack(tile, f):
        return pltpu.roll(tile, 128 - base_of(f), 1)

    def extend(first, count):
        fields = range(first, first + count)
        return [
            [own[first : first + count], jnp.stack([unpack(side_mid, f) for f in fields])],
            [
                jnp.where(
                    lax.broadcasted_iota(jnp.int32, (count, 8, 128), 1) < 4,
                    below[first : first + count],
                    above[first : first + count],
                ),
                jnp.stack([unpack(side_edge, f) for f in fields]),
            ],
        ]

    def each(f, *xs):
        return [[f(*[x[t][s] for x in xs]) for s in range(2)] for t in range(2)]

    def shift_rows(x, to, edge):
        r = each(lambda q: pltpu.roll(q, to % 8, 1), x)
        at = lax.broadcasted_iota(jnp.int32, x[0][0].shape, 1) == edge
        return [[jnp.where(at, r[1 - t][s], r[t][s]) for s in range(2)] for t in range(2)]

    def shift_cols(x, to, edge):
        r = each(lambda q: pltpu.roll(q, to % 128, 2), x)
        at = lax.broadcasted_iota(jnp.int32, x[0][0].shape, 2) == edge
        return [[jnp.where(at, r[t][1 - s], r[t][s]) for s in range(2)] for t in range(2)]

    def next_row(x):
        return shift_rows(x, -1, 7)

    def prev_row(x):
        return shift_rows(x, 1, 0)

    def next_col(x):
        return shift_cols(x, -1, 127)

    def prev_col(x):
        return shift_cols(x, 1, 0)

    def add(a, b):
        return each(lambda p, q: p + q, a, b)

    def four_sum(x):
        half = add(x, next_col(x))
        return add(half, next_row(half))

    def to_nodes(x):
        half = add(x, prev_row(x))
        return add(half, prev_col(half))

    u00 = extend(0, 6)
    u01 = next_col(u00)
    u10 = next_row(u00)
    at_three = lax.broadcasted_iota(jnp.int32, (6, 8, 128), 1) == 3
    u10[1] = [
        jnp.where(at_three, pltpu.roll(below[0:6], 7, 1), u10[1][0]),
        jnp.where(at_three, jnp.stack([unpack(side_next, f) for f in range(6)]), u10[1][1]),
    ]
    u11 = next_col(u10)
    corners = (u00, u01, u10, u11)
    field_mass, field_thick, field_added = extend(12, 1), extend(13, 1), extend(14, 1)
    forces = [[[None, None], [None, None]] for _ in range(4)]
    for t in range(2):
        stacked = jnp.concatenate(
            [
                jnp.concatenate([corners[n][t][s][c] for c in range(6) for n in range(4)], axis=0)
                for s in range(2)
            ],
            axis=1,
        )
        hi = stacked.astype(BF16)
        lo = (stacked - hi.astype(F32)).astype(BF16)
        product = (
            jnp.dot(big_hi, lo, preferred_element_type=F32)
            + jnp.dot(big_lo, hi, preferred_element_type=F32)
        ) + jnp.dot(big_hi, hi, preferred_element_type=F32)
        for n in range(4):
            for s in range(2):
                forces[n][t][s] = (
                    jnp.stack(
                        [
                            product[8 * (4 * c + n) : 8 * (4 * c + n) + 8, 128 * s : 128 * s + 128]
                            for c in range(6)
                        ]
                    )
                    * field_thick[t][s]
                )
    relay_step(3)
    internal = add(
        add(forces[0], prev_row(forces[2])), prev_col(add(forces[1], prev_row(forces[3])))
    )

    weight_sum = to_nodes(field_added)
    precond = each(lambda m, w: m + 0.75 * w, field_mass, weight_sum)
    inverse = each(lambda m: 1.0 / m, precond)
    quarter = each(lambda i: 0.25 * i, inverse)
    quarter_weight = each(lambda q, w: q * w, quarter, weight_sum)
    powers = [each(lambda f, g, i: (f - g) * i, extend(6, 6), internal, inverse)]
    for k in range(3):
        p = powers[-1]
        spread_sum = to_nodes(each(lambda a, s: a * s, field_added, four_sum(p)))
        powers.append(
            each(lambda q, n, w, v: q * n - w * v, quarter, spread_sum, quarter_weight, p)
        )

    mine = [x[0][0] for x in powers]
    weighted = [precond[0][0] * x for x in mine]
    moments = [jnp.sum(weighted[k // 2] * mine[k - k // 2], axis=0) for k in range(7)]
    last = four_sum(powers[3])[0][0]
    moments.append(
        0.25
        * jnp.sum(
            field_added[0][0] * (last * last) - weight_sum[0][0] * (mine[3] * mine[3]), axis=0
        )
    )
    sums = jnp.concatenate([jnp.sum(m, axis=0, keepdims=True) for m in moments], axis=0)
    sums = jnp.sum(sums, axis=1, keepdims=True)
    row = jnp.sum(jnp.where(row8 == lane8, sums, 0.0), axis=0, keepdims=True)

    around_mass = four_sum(field_mass)[0][0][0]
    stable = 0.5 * jnp.sqrt((weights[1] + 0.25 * around_mass) / weights[0])
    smallest = jnp.min(jnp.where(live > 0, stable, 1e30), keepdims=True)
    lane1 = lax.broadcasted_iota(jnp.int32, (1, 128), 1)
    row = jnp.where(lane1 == 8, smallest, row)

    for k in range(4, len(rounds) + 1):
        relay_step(k)

    def gather(row, size, here, src, slots, device, i):
        src[...] = row
        slots[pl.ds(here, 1)] = row.reshape(1, 1, 128)
        for k in range(1, size):
            pltpu.make_async_remote_copy(
                src_ref=src,
                dst_ref=slots.at[here],
                send_sem=red_send.at[i],
                recv_sem=red_recv.at[i],
                device_id=device(k),
                device_id_type=MESH,
            ).start()
        most = slots.at[pl.ds(0, size - 1)]
        pltpu.make_async_copy(most, most, red_recv.at[i]).wait()
        sums = [slots[k] for k in range(size)]
        lows = sums
        while len(sums) > 1:
            odd = len(sums) % 2
            sums, lows = (
                [sums[j] + sums[j + 1] for j in range(0, len(sums) - odd, 2)] + sums[len(sums) - odd :],
                [jnp.minimum(lows[j], lows[j + 1]) for j in range(0, len(lows) - odd, 2)]
                + lows[len(lows) - odd :],
            )
        return jnp.where(lane1 == 8, lows[0], sums[0])

    row = gather(row, n_py, py, row_plane, got_plane, lambda k: (px, at_py(k)), 0)
    row = gather(row, n_px, px, row_line, got_line, lambda k: (at_px(k), py), 1)

    row = jnp.broadcast_to(row, (8, 128))
    splat = [jnp.broadcast_to(row[:, k : k + 1], (8, 128)) for k in range(9)]
    accel = coefficients(splat[:8])
    min_step = splat[8]
    total = accel[0] * mine[0]
    for k in range(1, ITERS):
        total = total + accel[k] * mine[k]
    out_gain[...] = min_step * total
    out_step[...] = min_step

    pltpu.make_async_copy(strips, strips, halo_send.at[0]).wait()
    halo[6].wait_send()
    halo[7].wait_send()
    for i, (slots, size) in enumerate(((got_plane, n_py), (got_line, n_px))):
        most = slots.at[pl.ds(0, size - 1)]
        pltpu.make_async_copy(most, most, red_send.at[i]).wait()


def local(n_px, n_py, disp, vel, force, mass, thick, added, stiff, elements, counts):
    tiles = elements.shape[0]
    vmem = lambda *dims: pltpu.VMEM(dims, F32)
    dma = lambda n: pltpu.SemaphoreType.DMA((n,))
    gain, step = pl.pallas_call(
        functools.partial(kernel, n_px, n_py),
        out_shape=[jax.ShapeDtypeStruct(disp.shape, F32), jax.ShapeDtypeStruct((8, 128), F32)],
        in_specs=[pl.BlockSpec(memory_space=pltpu.HBM)] * 8,
        out_specs=[pl.BlockSpec(memory_space=pltpu.VMEM)] * 2,
        scratch_shapes=[
            vmem(FIELDS, 8, 128),
            vmem(2, 8, 128),
            vmem(24, 24),
            pltpu.VMEM((tiles, 128), jnp.int32),
            pltpu.VMEM((1, 1), jnp.int32),
            vmem(FIELDS, 8, 128),
            vmem(FIELDS, 8, 128),
            vmem(8, 128),
            vmem(6, 8, 128),
            vmem(1, 128),
            vmem(1, 128),
            vmem(n_py, 1, 128),
            vmem(n_px, 1, 128),
            dma(5),
            dma(3),
            dma(3),
            dma(2),
            dma(2),
            pltpu.SemaphoreType.REGULAR((4,)),
        ],
        compiler_params=pltpu.CompilerParams(collective_id=0, has_side_effects=True),
        name="crash_step",
    )(disp, force, mass, thick, added, stiff, elements, counts)
    new_velocity = vel + gain
    new_displacement = disp + step * new_velocity
    return new_velocity, new_displacement


def solution(mesh):
    field = P(None, "px", "py")
    plane = P("px", "py")
    return jax.shard_map(
        functools.partial(local, mesh.shape["px"], mesh.shape["py"]),
        mesh=mesh,
        in_specs=(field, field, field, plane, plane, plane, P(), plane, plane),
        out_specs=(field, field),
        check_vma=False,
    )
```

time: 38 us -> 38.3 us (level)
  local copies, waits for them, and re-layouts: 1.96 us -> 0.01 us
  other arithmetic: 0 us -> 1.37 us
  Pallas kernels: 34.5 us -> 35.3 us
    unnamed x4, local copies, waits for them, and re-layouts: 1.96 us -> 0.01 us
    add x0 -> x1, other arithmetic: none -> 1.37 us  [local(): new_displacement = disp + step * new_velocity]
    pallas_call x1, Pallas kernels: 34.5 us -> 35.3 us  [local(): pl.pallas_call(functools.partial(kernel, n_px, n_py), out_shape=[jax.Shap...]
where the time goes in v2:
time: 38.3 us; the launch traced here: 38 us
  Pallas kernels  35.3 us (92%)
  other arithmetic  1.37 us (4%)
  between operations  1.32 us (3%)
    pallas_call x1, Pallas kernels, local(): pl.pallas_call(functools.partial(kernel, n_px, n_py), out_shape=[jax.Shap...  35.3 us
    add x1, other arithmetic, local(): new_displacement = disp + step * new_velocity  1.37 us

profile of v2, /device:TPU:1, one launch (start us, length us, event | category | flops | bytes accessed | tf_op | source)
XLA Modules:
  0.0 38.0 jit_solution(6601100991786570040)
XLA Ops:
  1.3 0.0 copy-start
  1.3 0.0 copy-start.1
  1.3 35.3 %crash_step.1 = (f32[6,8,128]{2,1,0:T(8,128)}, f32[8,128]{1,0:T(8,128)}) custom-call(f32[6,8,128]{2,1,0:T(8,128)} %disp.1, f32[6,8,128]{2,1,0:T(8,128)} %force.1, f32[8,128]{1,0:T(8,128)} %mass.1, f32[8,128]{1,0:T(8,128)} %thick.1, f32[8,128]{1,0:T(8,128)} %added.1, f32[24,24]{1,0:T(8,128)} %stiff.1, s32[10,128]{1,0:T(8,128)} %elements.1, ...), custom_call_target="tpu_custom_call" | custom-call | tf_op jit(solution)/shard_map/crash_step/pallas_call | solution.py:434
  36.6 0.0 copy-done
  36.6 0.0 copy-done.1
  36.6 1.4 %multiply_add_fusion = (f32[6,8,128]{2,1,0:T(8,128)}, f32[6,8,128]{2,1,0:T(8,128)}) fusion(f32[6,8,128]{2,1,0:T(8,128)S(1)} %copy-done, f32[8,128]{1,0:T(8,128)} %get-tuple-element.5, f32[6,8,128]{2,1,0:T(8,128)S(1)} %copy-done.1, f32[6,8,128]{2,1,0:T(8,128)} %get-tuple-element.4), kind=kLoop, calls=%fused_computation | loop fusion | flops 18432 | bytes 126976 | tf_op jit(solution)/shard_map/add | solution.py:464
Async XLA Ops:
  1.3 35.3 %copy-start = (f32[6,8,128]{2,1,0:T(8,128)S(1)}, f32[6,8,128]{2,1,0:T(8,128)}, u32[]{:S(2)}) copy-start(f32[6,8,128]{2,1,0:T(8,128)} %disp.1) | copy-start | bytes 73732
  1.3 35.3 %copy-start.1 = (f32[6,8,128]{2,1,0:T(8,128)S(1)}, f32[6,8,128]{2,1,0:T(8,128)}, u32[]{:S(2)}) copy-start(f32[6,8,128]{2,1,0:T(8,128)} %param.10) | copy-start | bytes 73732

commit v3 on v2

--- a/solution.py
+++ b/solution.py
@@ -117,9 +117,15 @@
     def signal(sem, a, b):
         pl.semaphore_signal(sem, inc=1, device_id=(a, b), device_id_type=MESH)
 
-    around = [(up, left), (up, py), (up, right), (px, left), (px, right), (down, left), (down, py), (down, right)]
-    for a, b in around:
-        signal(barrier, a, b)
+    span = n_py // 4 if n_py >= 8 else n_py
+    start = lax.div(py, span) * span
+    row_peers = [start + lax.rem(py - start + k, span) for k in range(1, span)]
+    column_peers = [at_py(k) for k in range(span, n_py, span)]
+    for a in (up, down):
+        for b in (left, right, py):
+            signal(barrier, a, b)
+    for b in [left, right] + column_peers + row_peers:
+        signal(barrier, px, b)
 
     row8 = lax.broadcasted_iota(jnp.int32, (8, 128), 0)
     lane8 = lax.broadcasted_iota(jnp.int32, (8, 128), 1)
@@ -164,7 +170,7 @@
         packed = jnp.where(lane_group == f, pltpu.roll(own[f], base_of(f), 1), packed)
     strip_out[...] = packed
 
-    pl.semaphore_wait(barrier, 8)
+    pl.semaphore_wait(barrier, 8 + len(row_peers) + len(column_peers))
 
     halo = [
         pltpu.make_async_remote_copy(
@@ -189,31 +195,20 @@
     for copy in halo:
         copy.start()
 
-    def tell(k, axes):
-        far = 1 << k
-        if "px" in axes:
-            signal(relay.at[k], at_px(far), py)
-            signal(relay.at[k], at_px(-far), py)
-        if "py" in axes:
-            signal(relay.at[k], px, at_py(far))
-            signal(relay.at[k], px, at_py(-far))
-
-    rounds = []
-    far = 1
-    while 2 * far <= max(n_px, n_py) // 2:
-        rounds.append([n for n, size in (("px", n_px), ("py", n_py)) if 2 * far <= size // 2])
-        far *= 2
-
-    def listen(k):
-        pl.semaphore_wait(relay.at[k], 2 * len(rounds[k]))
-
-    def relay_step(k):
-        if 1 <= k <= len(rounds):
-            listen(k - 1)
-        if k < len(rounds):
-            tell(k, rounds[k])
-
-    relay_step(0)
+    for b in column_peers:
+        signal(relay.at[0], px, b)
+    rounds = 0
+    while 2 << rounds <= n_px // 2:
+        rounds += 1
+
+    def pass_on(k):
+        if 1 <= k <= rounds:
+            pl.semaphore_wait(relay.at[k], 2)
+        if k < rounds:
+            signal(relay.at[k + 1], at_px(1 << k), py)
+            signal(relay.at[k + 1], at_px(-(1 << k)), py)
+
+    pass_on(0)
 
     loads[7].wait()
     spread = jnp.where(
@@ -236,8 +231,7 @@
     stiff_lo = (stiff_all - stiff_hi.astype(F32)).astype(BF16)
     big_hi, big_lo = expand(stiff_hi), expand(stiff_lo)
 
-    relay_step(1)
-    relay_step(2)
+    pass_on(1)
 
     pltpu.make_async_copy(strips, strips, halo_recv.at[0]).wait()
     halo[6].wait_recv()
@@ -340,7 +334,7 @@
                     )
                     * field_thick[t][s]
                 )
-    relay_step(3)
+    pass_on(2)
     internal = add(
         add(forces[0], prev_row(forces[2])), prev_col(add(forces[1], prev_row(forces[3])))
     )
@@ -378,13 +372,13 @@
     lane1 = lax.broadcasted_iota(jnp.int32, (1, 128), 1)
     row = jnp.where(lane1 == 8, smallest, row)
 
-    for k in range(4, len(rounds) + 1):
-        relay_step(k)
-
-    def gather(row, size, here, src, slots, device, i):
+    if column_peers:
+        pl.semaphore_wait(relay.at[0], len(column_peers))
+
+    def gather(row, size, here, src, slots, device, far, i):
         src[...] = row
         slots[pl.ds(here, 1)] = row.reshape(1, 1, 128)
-        for k in range(1, size):
+        for k in sorted(range(1, size), key=far):
             pltpu.make_async_remote_copy(
                 src_ref=src,
                 dst_ref=slots.at[here],
@@ -406,8 +400,17 @@
             )
         return jnp.where(lane1 == 8, lows[0], sums[0])
 
-    row = gather(row, n_py, py, row_plane, got_plane, lambda k: (px, at_py(k)), 0)
-    row = gather(row, n_px, px, row_line, got_line, lambda k: (at_px(k), py), 1)
+    def line_far(k):
+        return -min(k, n_px - k)
+
+    def plane_far(k):
+        x, y = k // 2 % 4, k // 8
+        return -(min(x, 4 - x) + min(y, 4 - y))
+
+    row = gather(row, n_py, py, row_plane, got_plane, lambda k: (px, at_py(k)), plane_far, 0)
+    for k in range(3, rounds + 1):
+        pass_on(k)
+    row = gather(row, n_px, px, row_line, got_line, lambda k: (at_px(k), py), line_far, 1)
 
     row = jnp.broadcast_to(row, (8, 128))
     splat = [jnp.broadcast_to(row[:, k : k + 1], (8, 128)) for k in range(9)]
@@ -457,9 +460,11 @@
             dma(2),
             pltpu.SemaphoreType.REGULAR((4,)),
         ],
-        compiler_params=pltpu.CompilerParams(collective_id=0, has_side_effects=True),
+        compiler_params=pltpu.CompilerParams(
+            collective_id=0, has_side_effects=True, vmem_limit_bytes=8 << 20
+        ),
         name="crash_step",
-    )(disp, force, mass, thick, added, stiff, elements, counts)
+    )(*(pltpu.with_memory_space_constraint(x, pltpu.HBM) for x in (disp, force, mass, thick, added, stiff, elements)), counts)
     new_velocity = vel + gain
     new_displacement = disp + step * new_velocity
     return new_velocity, new_displacement

time: 38.3 us -> 34.5 us (0.901)
  Pallas kernels: 35.3 us -> 32.3 us
  other arithmetic: 1.37 us -> 0.63 us
    pallas_call x1, Pallas kernels: 35.3 us -> 32.3 us  [local(): pl.pallas_call(functools.partial(kernel, n_px, n_py), out_shape=[jax.Shap...]
    add x1, other arithmetic: 1.37 us -> 0.63 us  [local(): new_displacement = disp + step * new_velocity]
where the time goes in v3:
time: 34.5 us; the launch traced here: 34.2 us
  Pallas kernels  32.3 us (94%)
  between operations  1.32 us (4%)
  other arithmetic  0.63 us (2%)
    pallas_call x1, Pallas kernels, local(): pl.pallas_call(functools.partial(kernel, n_px, n_py), out_shape=[jax.Shap...  32.3 us

profile of v3, /device:TPU:1, one launch (start us, length us, event | category | flops | bytes accessed | tf_op | source)
XLA Modules:
  0.0 34.2 jit_solution(3251445621019987773)
XLA Ops:
  1.3 0.0 copy-start
  1.3 0.0 copy-start.1
  1.3 32.3 %crash_step.1 = (f32[6,8,128]{2,1,0:T(8,128)S(1)}, f32[8,128]{1,0:T(8,128)S(1)}) custom-call(f32[6,8,128]{2,1,0:T(8,128)} %disp.1, f32[6,8,128]{2,1,0:T(8,128)} %force.1, f32[8,128]{1,0:T(8,128)} %mass.1, f32[8,128]{1,0:T(8,128)} %thick.1, f32[8,128]{1,0:T(8,128)} %added.1, f32[24,24]{1,0:T(8,128)} %stiff.1, s32[10,128]{1,0:T(8,128)} %elements.1, ...), custom_call_target="tpu_custom_call" | custom-call | tf_op jit(solution)/shard_map/crash_step/pallas_call | solution.py:437
  33.6 0.0 copy-done
  33.6 0.0 copy-done.1
  33.6 0.6 %multiply_add_fusion = (f32[6,8,128]{2,1,0:T(8,128)}, f32[6,8,128]{2,1,0:T(8,128)}) fusion(f32[6,8,128]{2,1,0:T(8,128)S(1)} %copy-done, f32[8,128]{1,0:T(8,128)S(1)} %get-tuple-element.5, f32[6,8,128]{2,1,0:T(8,128)S(1)} %copy-done.1, f32[6,8,128]{2,1,0:T(8,128)S(1)} %get-tuple-element.4), kind=kLoop, calls=%fused_computation | loop fusion | flops 18432 | bytes 126976 | tf_op jit(solution)/shard_map/add | solution.py:469
Async XLA Ops:
  1.3 32.3 %copy-start = (f32[6,8,128]{2,1,0:T(8,128)S(1)}, f32[6,8,128]{2,1,0:T(8,128)}, u32[]{:S(2)}) copy-start(f32[6,8,128]{2,1,0:T(8,128)} %disp.1) | copy-start | bytes 73732
  1.3 32.3 %copy-start.1 = (f32[6,8,128]{2,1,0:T(8,128)S(1)}, f32[6,8,128]{2,1,0:T(8,128)}, u32[]{:S(2)}) copy-start(f32[6,8,128]{2,1,0:T(8,128)} %param.10) | copy-start | bytes 73732

commit v4 on v3

--- a/solution.py
+++ b/solution.py
@@ -70,7 +70,6 @@
     weights,
     stiff_v,
     elem_v,
-    count_v,
     above,
     below,
     strip_out,
@@ -99,13 +98,12 @@
         pltpu.make_async_copy(src, dst, in_sem.at[i])
         for src, dst, i in (
             (elements, elem_v, 0),
-            (counts, count_v, 1),
-            (thick, weights.at[0], 2),
-            (added, weights.at[1], 2),
-            (disp, own.at[0:6], 3),
-            (force, own.at[6:12], 3),
-            (mass, own.at[12], 3),
-            (stiff, stiff_v, 4),
+            (thick, weights.at[0], 1),
+            (added, weights.at[1], 1),
+            (disp, own.at[0:6], 2),
+            (force, own.at[6:12], 2),
+            (mass, own.at[12], 2),
+            (stiff, stiff_v, 3),
         )
     ]
     for load in loads:
@@ -122,8 +120,7 @@
     row_peers = [start + lax.rem(py - start + k, span) for k in range(1, span)]
     column_peers = [at_py(k) for k in range(span, n_py, span)]
     for a in (up, down):
-        for b in (left, right, py):
-            signal(barrier, a, b)
+        signal(barrier, a, py)
     for b in [left, right] + column_peers + row_peers:
         signal(barrier, px, b)
 
@@ -131,7 +128,6 @@
     lane8 = lax.broadcasted_iota(jnp.int32, (8, 128), 1)
 
     loads[0].wait()
-    loads[1].wait()
     ids = elem_v[...]
     tiles = ids.shape[0]
     slot = lax.broadcasted_iota(jnp.int32, (tiles, 128), 0) * 128 + lax.broadcasted_iota(
@@ -139,7 +135,7 @@
     )
     id_row = lax.shift_right_logical(ids * 4033, 19)
     id_col = ids - id_row * 130
-    id_row = jnp.where(slot < count_v[...], id_row, -1)
+    id_row = jnp.where(slot < counts[0, 0], id_row, -1)
     row_sel = row8 + 1
     col_sel = lax.broadcasted_iota(jnp.int32, (128, 128), 0) + 1
     hot_rows, hot_cols = [], []
@@ -156,11 +152,11 @@
         (((1,), (1,)), ((), ())),
         preferred_element_type=F32,
     )
-    pltpu.make_async_copy(weights, weights, in_sem.at[2]).wait()
+    pltpu.make_async_copy(weights, weights, in_sem.at[1]).wait()
     own[13] = weights[0] * live
     own[14] = weights[1] * live
 
-    pltpu.make_async_copy(own.at[0:13], own.at[0:13], in_sem.at[3]).wait()
+    pltpu.make_async_copy(own.at[0:13], own.at[0:13], in_sem.at[2]).wait()
     lane_group = jnp.where(
         lane8 < 54, lax.shift_right_logical(lane8 * 57, 9), lax.shift_right_logical(lane8 - 54, 3) + 6
     )
@@ -170,10 +166,10 @@
         packed = jnp.where(lane_group == f, pltpu.roll(own[f], base_of(f), 1), packed)
     strip_out[...] = packed
 
-    pl.semaphore_wait(barrier, 8 + len(row_peers) + len(column_peers))
-
-    halo = [
-        pltpu.make_async_remote_copy(
+    pl.semaphore_wait(barrier, 4 + len(row_peers) + len(column_peers))
+
+    def remote(src, dst, a, b, i):
+        return pltpu.make_async_remote_copy(
             src_ref=src,
             dst_ref=dst,
             send_sem=halo_send.at[i],
@@ -181,18 +177,16 @@
             device_id=(a, b),
             device_id_type=MESH,
         )
-        for src, dst, a, b, i in (
-            (strip_out, strips.at[2], down, right, 0),
-            (strip_out, strips.at[3], down, left, 0),
-            (strip_out, strips.at[4], up, right, 0),
-            (strip_out, strips.at[5], up, left, 0),
-            (strip_out, strips.at[0], px, right, 0),
-            (strip_out, strips.at[1], px, left, 0),
-            (own.at[:, 4:8, :], above.at[:, 4:8, :], down, py, 1),
-            (own.at[:, 0:5, :], below.at[:, 0:5, :], up, py, 2),
-        )
+
+    halo = [
+        remote(strip_out, strips.at[0], px, right, 0),
+        remote(strip_out, strips.at[1], px, left, 1),
+        remote(own.at[:, 4:8, :], above.at[:, 4:8, :], down, py, 2),
+        remote(own.at[:, 0:5, :], below.at[:, 0:5, :], up, py, 3),
+        remote(strips.at[0:2], strips.at[2:4], down, py, 4),
+        remote(strips.at[0:2], strips.at[4:6], up, py, 5),
     ]
-    for copy in halo:
+    for copy in halo[:4]:
         copy.start()
 
     for b in column_peers:
@@ -210,7 +204,7 @@
 
     pass_on(0)
 
-    loads[7].wait()
+    loads[6].wait()
     spread = jnp.where(
         lax.shift_right_logical(lax.broadcasted_iota(jnp.int32, (192, 24), 0), 3)
         == lax.broadcasted_iota(jnp.int32, (192, 24), 1),
@@ -233,9 +227,12 @@
 
     pass_on(1)
 
-    pltpu.make_async_copy(strips, strips, halo_recv.at[0]).wait()
-    halo[6].wait_recv()
-    halo[7].wait_recv()
+    halo[0].wait_recv()
+    halo[1].wait_recv()
+    for copy in halo[4:]:
+        copy.start()
+    for copy in halo[2:]:
+        copy.wait_recv()
 
     lower = row8 < 4
     side_mid = jnp.where(from_left, strips[0], strips[1])
@@ -422,9 +419,8 @@
     out_gain[...] = min_step * total
     out_step[...] = min_step
 
-    pltpu.make_async_copy(strips, strips, halo_send.at[0]).wait()
-    halo[6].wait_send()
-    halo[7].wait_send()
+    for copy in halo:
+        copy.wait_send()
     for i, (slots, size) in enumerate(((got_plane, n_py), (got_line, n_px))):
         most = slots.at[pl.ds(0, size - 1)]
         pltpu.make_async_copy(most, most, red_send.at[i]).wait()
@@ -437,14 +433,13 @@
     gain, step = pl.pallas_call(
         functools.partial(kernel, n_px, n_py),
         out_shape=[jax.ShapeDtypeStruct(disp.shape, F32), jax.ShapeDtypeStruct((8, 128), F32)],
-        in_specs=[pl.BlockSpec(memory_space=pltpu.HBM)] * 8,
+        in_specs=[pl.BlockSpec(memory_space=pltpu.HBM)] * 7 + [pl.BlockSpec(memory_space=pltpu.SMEM)],
         out_specs=[pl.BlockSpec(memory_space=pltpu.VMEM)] * 2,
         scratch_shapes=[
             vmem(FIELDS, 8, 128),
             vmem(2, 8, 128),
             vmem(24, 24),
             pltpu.VMEM((tiles, 128), jnp.int32),
-            pltpu.VMEM((1, 1), jnp.int32),
             vmem(FIELDS, 8, 128),
             vmem(FIELDS, 8, 128),
             vmem(8, 128),
@@ -453,9 +448,9 @@
             vmem(1, 128),
             vmem(n_py, 1, 128),
             vmem(n_px, 1, 128),
-            dma(5),
-            dma(3),
-            dma(3),
+            dma(4),
+            dma(6),
+            dma(6),
             dma(2),
             dma(2),
             pltpu.SemaphoreType.REGULAR((4,)),

time: 34.5 us -> 34.1 us (0.988)
  no operation moved by 1% of the time
where the time goes in v4:
time: 34.1 us; the launch traced here: 33.9 us
  Pallas kernels  32 us (94%)
  between operations  1.32 us (4%)
  other arithmetic  0.63 us (2%)
    pallas_call x1, Pallas kernels, local(): pl.pallas_call(functools.partial(kernel, n_px, n_py), out_shape=[jax.Shap...  32 us

profile of v4, /device:TPU:1, one launch (start us, length us, event | category | flops | bytes accessed | tf_op | source)
XLA Modules:
  0.0 33.9 jit_solution(13160426299374494733)
XLA Ops:
  1.3 0.0 copy-start
  1.3 0.0 copy-start.1
  1.3 32.0 %crash_step.1 = (f32[6,8,128]{2,1,0:T(8,128)S(1)}, f32[8,128]{1,0:T(8,128)S(1)}) custom-call(f32[6,8,128]{2,1,0:T(8,128)} %disp.1, f32[6,8,128]{2,1,0:T(8,128)} %force.1, f32[8,128]{1,0:T(8,128)} %mass.1, f32[8,128]{1,0:T(8,128)} %thick.1, f32[8,128]{1,0:T(8,128)} %added.1, f32[24,24]{1,0:T(8,128)} %stiff.1, s32[10,128]{1,0:T(8,128)} %elements.1, ...), custom_call_target="tpu_custom_call" | custom-call | tf_op jit(solution)/shard_map/crash_step/pallas_call | solution.py:433
  33.3 0.0 copy-done
  33.3 0.0 copy-done.1
  33.3 0.6 %multiply_add_fusion = (f32[6,8,128]{2,1,0:T(8,128)}, f32[6,8,128]{2,1,0:T(8,128)}) fusion(f32[6,8,128]{2,1,0:T(8,128)S(1)} %copy-done, f32[8,128]{1,0:T(8,128)S(1)} %get-tuple-element.5, f32[6,8,128]{2,1,0:T(8,128)S(1)} %copy-done.1, f32[6,8,128]{2,1,0:T(8,128)S(1)} %get-tuple-element.4), kind=kLoop, calls=%fused_computation | loop fusion | flops 18432 | bytes 126976 | tf_op jit(solution)/shard_map/add | solution.py:464
Async XLA Ops:
  1.3 32.0 %copy-start = (f32[6,8,128]{2,1,0:T(8,128)S(1)}, f32[6,8,128]{2,1,0:T(8,128)}, u32[]{:S(2)}) copy-start(f32[6,8,128]{2,1,0:T(8,128)} %disp.1) | copy-start | bytes 73732
  1.3 32.0 %copy-start.1 = (f32[6,8,128]{2,1,0:T(8,128)S(1)}, f32[6,8,128]{2,1,0:T(8,128)}, u32[]{:S(2)}) copy-start(f32[6,8,128]{2,1,0:T(8,128)} %param.10) | copy-start | bytes 73732

commit v5 on v4

--- a/solution.py
+++ b/solution.py
@@ -49,8 +49,12 @@
     return accel
 
 
-def base_of(f):
-    return 9 * f + 4 if f < 6 else 54 + 8 * (f - 6) + 4
+def width_of(f):
+    return 9 if f < 6 or f > 12 else 8
+
+
+ORDER = [0, 1, 2, 3, 4, 5, 13, 14, 6, 7, 8, 9, 10, 11, 12]
+BASE = {f: sum(width_of(g) for g in ORDER[: ORDER.index(f)]) for f in ORDER}
 
 
 def kernel(
@@ -73,7 +77,8 @@
     above,
     below,
     strip_out,
-    strips,
+    strips_left,
+    strips_right,
     row_plane,
     row_line,
     got_plane,
@@ -116,12 +121,22 @@
         pl.semaphore_signal(sem, inc=1, device_id=(a, b), device_id_type=MESH)
 
     span = n_py // 4 if n_py >= 8 else n_py
-    start = lax.div(py, span) * span
-    row_peers = [start + lax.rem(py - start + k, span) for k in range(1, span)]
-    column_peers = [at_py(k) for k in range(span, n_py, span)]
+    n_x, n_y = span // 2, n_py // span
+    core, chip_x, chip_y = lax.rem(py, 2), lax.div(lax.rem(py, span), 2), lax.div(py, span)
+
+    def in_plane(dx, dy, other=False):
+        x = lax.rem(chip_x + (n_x + dx), n_x)
+        y = lax.rem(chip_y + (n_y + dy), n_y)
+        return y * span + x * 2 + (1 - core if other else core)
+
+    row_peers = [in_plane(1, 0), in_plane(-1, 0)]
+    column_peers = [in_plane(0, 1), in_plane(0, -1)] if n_y > 1 else []
+    beside = row_peers + [in_plane(1, 0, True), in_plane(-1, 0, True)] + column_peers
+    signal(barrier, px, right)
+    signal(barrier, px, left)
     for a in (up, down):
         signal(barrier, a, py)
-    for b in [left, right] + column_peers + row_peers:
+    for b in beside:
         signal(barrier, px, b)
 
     row8 = lax.broadcasted_iota(jnp.int32, (8, 128), 0)
@@ -157,16 +172,21 @@
     own[14] = weights[1] * live
 
     pltpu.make_async_copy(own.at[0:13], own.at[0:13], in_sem.at[2]).wait()
-    lane_group = jnp.where(
-        lane8 < 54, lax.shift_right_logical(lane8 * 57, 9), lax.shift_right_logical(lane8 - 54, 3) + 6
-    )
-    from_left = jnp.where(lane8 < 54, lane8 - 9 * lane_group, (lane8 - 54) & 7) < 4
-    packed = jnp.zeros((8, 128), F32)
+    to_right = jnp.zeros((8, 128), F32)
+    to_left = jnp.zeros((8, 128), F32)
     for f in range(FIELDS):
-        packed = jnp.where(lane_group == f, pltpu.roll(own[f], base_of(f), 1), packed)
-    strip_out[...] = packed
-
-    pl.semaphore_wait(barrier, 4 + len(row_peers) + len(column_peers))
+        field = own[f]
+        start, end = BASE[f], BASE[f] + width_of(f)
+        to_right = jnp.where(
+            (lane8 >= start) & (lane8 < end), pltpu.roll(field, end % 128, 1), to_right
+        )
+        to_left = jnp.where(
+            (lane8 >= 5 * f) & (lane8 < 5 * f + 5), pltpu.roll(field, 5 * f, 1), to_left
+        )
+    strip_out[0] = to_right
+    strip_out[1] = to_left
+
+    pl.semaphore_wait(barrier, 4 + len(beside))
 
     def remote(src, dst, a, b, i):
         return pltpu.make_async_remote_copy(
@@ -179,28 +199,39 @@
         )
 
     halo = [
-        remote(strip_out, strips.at[0], px, right, 0),
-        remote(strip_out, strips.at[1], px, left, 1),
-        remote(own.at[:, 4:8, :], above.at[:, 4:8, :], down, py, 2),
-        remote(own.at[:, 0:5, :], below.at[:, 0:5, :], up, py, 3),
-        remote(strips.at[0:2], strips.at[2:4], down, py, 4),
-        remote(strips.at[0:2], strips.at[4:6], up, py, 5),
+        remote(strip_out.at[0], strips_left.at[0], px, right, 0),
+        remote(own.at[:, 4:8, :], above.at[:, 4:8, :], down, py, 1),
+        remote(own.at[:, 0:5, :], below.at[:, 0:5, :], up, py, 2),
+        remote(strip_out.at[1], strips_right.at[0], px, left, 3),
+        remote(strips_left.at[0], strips_left.at[1], down, py, 4),
+        remote(strips_left.at[0], strips_left.at[2], up, py, 5),
+        remote(strips_right.at[0], strips_right.at[1], down, py, 6),
+        remote(strips_right.at[0], strips_right.at[2], up, py, 7),
     ]
     for copy in halo[:4]:
         copy.start()
 
-    for b in column_peers:
-        signal(relay.at[0], px, b)
+    def plane_round(k):
+        if k >= 1 and (k == 1 or column_peers):
+            pl.semaphore_wait(relay.at[k - 1], 2)
+        if k == 0:
+            for b in row_peers:
+                signal(relay.at[0], px, b)
+        elif k < 3:
+            for b in column_peers:
+                signal(relay.at[k], px, b)
+
+    plane_round(0)
     rounds = 0
     while 2 << rounds <= n_px // 2:
         rounds += 1
 
     def pass_on(k):
         if 1 <= k <= rounds:
-            pl.semaphore_wait(relay.at[k], 2)
+            pl.semaphore_wait(relay.at[2 + k], 2)
         if k < rounds:
-            signal(relay.at[k + 1], at_px(1 << k), py)
-            signal(relay.at[k + 1], at_px(-(1 << k)), py)
+            signal(relay.at[3 + k], at_px(1 << k), py)
+            signal(relay.at[3 + k], at_px(-(1 << k)), py)
 
     pass_on(0)
 
@@ -226,35 +257,40 @@
     big_hi, big_lo = expand(stiff_hi), expand(stiff_lo)
 
     pass_on(1)
+    plane_round(1)
 
     halo[0].wait_recv()
-    halo[1].wait_recv()
-    for copy in halo[4:]:
-        copy.start()
-    for copy in halo[2:]:
-        copy.wait_recv()
+    halo[4].start()
+    halo[5].start()
+    plane_round(2)
+    for i in (1, 2, 4, 5):
+        halo[i].wait_recv()
 
     lower = row8 < 4
-    side_mid = jnp.where(from_left, strips[0], strips[1])
-    side_above = jnp.where(from_left, strips[2], strips[3])
-    side_below = jnp.where(from_left, strips[4], strips[5])
-    side_edge = jnp.where(lower, side_below, side_above)
-    side_next = pltpu.roll(side_below, 7, 0)
-
-    def unpack(tile, f):
-        return pltpu.roll(tile, 128 - base_of(f), 1)
+
+    def edges(strips):
+        return strips[0], jnp.where(lower, strips[2], strips[1]), pltpu.roll(strips[2], 7, 0)
+
+    lefts = edges(strips_left)
+    rights = None
+
+    def side(i, f):
+        column = pltpu.roll(lefts[i], (128 - BASE[f] - width_of(f)) % 128, 1)
+        if rights is not None:
+            column = jnp.where(lane8 < 5, pltpu.roll(rights[i], (128 - 5 * f) % 128, 1), column)
+        return column
 
     def extend(first, count):
         fields = range(first, first + count)
         return [
-            [own[first : first + count], jnp.stack([unpack(side_mid, f) for f in fields])],
+            [own[first : first + count], jnp.stack([side(0, f) for f in fields])],
             [
                 jnp.where(
                     lax.broadcasted_iota(jnp.int32, (count, 8, 128), 1) < 4,
                     below[first : first + count],
                     above[first : first + count],
                 ),
-                jnp.stack([unpack(side_edge, f) for f in fields]),
+                jnp.stack([side(1, f) for f in fields]),
             ],
         ]
 
@@ -294,85 +330,91 @@
         half = add(x, prev_row(x))
         return add(half, prev_col(half))
 
-    u00 = extend(0, 6)
-    u01 = next_col(u00)
-    u10 = next_row(u00)
-    at_three = lax.broadcasted_iota(jnp.int32, (6, 8, 128), 1) == 3
-    u10[1] = [
-        jnp.where(at_three, pltpu.roll(below[0:6], 7, 1), u10[1][0]),
-        jnp.where(at_three, jnp.stack([unpack(side_next, f) for f in range(6)]), u10[1][1]),
-    ]
-    u11 = next_col(u10)
-    corners = (u00, u01, u10, u11)
-    field_mass, field_thick, field_added = extend(12, 1), extend(13, 1), extend(14, 1)
-    forces = [[[None, None], [None, None]] for _ in range(4)]
-    for t in range(2):
-        stacked = jnp.concatenate(
-            [
-                jnp.concatenate([corners[n][t][s][c] for c in range(6) for n in range(4)], axis=0)
-                for s in range(2)
-            ],
-            axis=1,
-        )
-        hi = stacked.astype(BF16)
-        lo = (stacked - hi.astype(F32)).astype(BF16)
-        product = (
-            jnp.dot(big_hi, lo, preferred_element_type=F32)
-            + jnp.dot(big_lo, hi, preferred_element_type=F32)
-        ) + jnp.dot(big_hi, hi, preferred_element_type=F32)
-        for n in range(4):
-            for s in range(2):
-                forces[n][t][s] = (
-                    jnp.stack(
-                        [
-                            product[8 * (4 * c + n) : 8 * (4 * c + n) + 8, 128 * s : 128 * s + 128]
-                            for c in range(6)
-                        ]
+    def solve():
+        u00 = extend(0, 6)
+        u01 = next_col(u00)
+        u10 = next_row(u00)
+        at_three = lax.broadcasted_iota(jnp.int32, (6, 8, 128), 1) == 3
+        u10[1] = [
+            jnp.where(at_three, pltpu.roll(below[0:6], 7, 1), u10[1][0]),
+            jnp.where(at_three, jnp.stack([side(2, f) for f in range(6)]), u10[1][1]),
+        ]
+        u11 = next_col(u10)
+        corners = (u00, u01, u10, u11)
+        field_mass, field_thick, field_added = extend(12, 1), extend(13, 1), extend(14, 1)
+        forces = [[[None, None], [None, None]] for _ in range(4)]
+        for t in range(2):
+            stacked = jnp.concatenate(
+                [
+                    jnp.concatenate([corners[n][t][s][c] for c in range(6) for n in range(4)], axis=0)
+                    for s in range(2)
+                ],
+                axis=1,
+            )
+            hi = stacked.astype(BF16)
+            lo = (stacked - hi.astype(F32)).astype(BF16)
+            product = (
+                jnp.dot(big_hi, lo, preferred_element_type=F32)
+                + jnp.dot(big_lo, hi, preferred_element_type=F32)
+            ) + jnp.dot(big_hi, hi, preferred_element_type=F32)
+            for n in range(4):
+                for s in range(2):
+                    forces[n][t][s] = (
+                        jnp.stack(
+                            [
+                                product[8 * (4 * c + n) : 8 * (4 * c + n) + 8, 128 * s : 128 * s + 128]
+                                for c in range(6)
+                            ]
+                        )
+                        * field_thick[t][s]
                     )
-                    * field_thick[t][s]
-                )
+        internal = add(
+            add(forces[0], prev_row(forces[2])), prev_col(add(forces[1], prev_row(forces[3])))
+        )
+
+        weight_sum = to_nodes(field_added)
+        precond = each(lambda m, w: m + 0.75 * w, field_mass, weight_sum)
+        inverse = each(lambda m: 1.0 / m, precond)
+        quarter = each(lambda i: 0.25 * i, inverse)
+        quarter_weight = each(lambda q, w: q * w, quarter, weight_sum)
+        powers = [each(lambda f, g, i: (f - g) * i, extend(6, 6), internal, inverse)]
+        for k in range(3):
+            p = powers[-1]
+            spread_sum = to_nodes(each(lambda a, s: a * s, field_added, four_sum(p)))
+            powers.append(
+                each(lambda q, n, w, v: q * n - w * v, quarter, spread_sum, quarter_weight, p)
+            )
+        return powers, precond, weight_sum, field_mass, field_thick, field_added
+
+    powers, precond, weight_sum, field_mass, field_thick, field_added = solve()
     pass_on(2)
-    internal = add(
-        add(forces[0], prev_row(forces[2])), prev_col(add(forces[1], prev_row(forces[3])))
-    )
-
-    weight_sum = to_nodes(field_added)
-    precond = each(lambda m, w: m + 0.75 * w, field_mass, weight_sum)
-    inverse = each(lambda m: 1.0 / m, precond)
-    quarter = each(lambda i: 0.25 * i, inverse)
-    quarter_weight = each(lambda q, w: q * w, quarter, weight_sum)
-    powers = [each(lambda f, g, i: (f - g) * i, extend(6, 6), internal, inverse)]
-    for k in range(3):
-        p = powers[-1]
-        spread_sum = to_nodes(each(lambda a, s: a * s, field_added, four_sum(p)))
-        powers.append(
-            each(lambda q, n, w, v: q * n - w * v, quarter, spread_sum, quarter_weight, p)
-        )
-
-    mine = [x[0][0] for x in powers]
-    weighted = [precond[0][0] * x for x in mine]
-    moments = [jnp.sum(weighted[k // 2] * mine[k - k // 2], axis=0) for k in range(7)]
-    last = four_sum(powers[3])[0][0]
+
+    def range_of(x):
+        return jnp.where(lax.broadcasted_iota(jnp.int32, x[0][0].shape, 2) < 123, x[0][0], x[0][1])
+
+    part = [range_of(x) for x in powers]
+    mass_part, sum_part, added_part = range_of(precond), range_of(weight_sum), range_of(field_added)
+    weighted = [mass_part * x for x in part]
+    moments = [jnp.sum(weighted[k // 2] * part[k - k // 2], axis=0) for k in range(7)]
+    last = range_of(four_sum(powers[3]))
     moments.append(
-        0.25
-        * jnp.sum(
-            field_added[0][0] * (last * last) - weight_sum[0][0] * (mine[3] * mine[3]), axis=0
-        )
+        0.25 * jnp.sum(added_part * (last * last) - sum_part * (part[3] * part[3]), axis=0)
     )
     sums = jnp.concatenate([jnp.sum(m, axis=0, keepdims=True) for m in moments], axis=0)
     sums = jnp.sum(sums, axis=1, keepdims=True)
     row = jnp.sum(jnp.where(row8 == lane8, sums, 0.0), axis=0, keepdims=True)
 
-    around_mass = four_sum(field_mass)[0][0][0]
-    stable = 0.5 * jnp.sqrt((weights[1] + 0.25 * around_mass) / weights[0])
-    smallest = jnp.min(jnp.where(live > 0, stable, 1e30), keepdims=True)
+    added_part = added_part[0]
+    stable = 0.5 * jnp.sqrt(
+        (added_part + 0.25 * range_of(four_sum(field_mass))[0]) / range_of(field_thick)[0]
+    )
+    smallest = jnp.min(jnp.where(added_part > 0, stable, 1e30), keepdims=True)
     lane1 = lax.broadcasted_iota(jnp.int32, (1, 128), 1)
     row = jnp.where(lane1 == 8, smallest, row)
 
-    if column_peers:
-        pl.semaphore_wait(relay.at[0], len(column_peers))
-
-    def gather(row, size, here, src, slots, device, far, i):
+    plane_round(3)
+
+    def spread_row(row, size, here, src, slots, device, far, i):
         src[...] = row
         slots[pl.ds(here, 1)] = row.reshape(1, 1, 128)
         for k in sorted(range(1, size), key=far):
@@ -384,6 +426,8 @@
                 device_id=device(k),
                 device_id_type=MESH,
             ).start()
+
+    def collect(size, slots, i):
         most = slots.at[pl.ds(0, size - 1)]
         pltpu.make_async_copy(most, most, red_recv.at[i]).wait()
         sums = [slots[k] for k in range(size)]
@@ -404,10 +448,20 @@
         x, y = k // 2 % 4, k // 8
         return -(min(x, 4 - x) + min(y, 4 - y))
 
-    row = gather(row, n_py, py, row_plane, got_plane, lambda k: (px, at_py(k)), plane_far, 0)
+    spread_row(row, n_py, py, row_plane, got_plane, lambda k: (px, at_py(k)), plane_far, 0)
+    halo[3].wait_recv()
+    halo[6].start()
+    halo[7].start()
+    row = collect(n_py, got_plane, 0)
     for k in range(3, rounds + 1):
         pass_on(k)
-    row = gather(row, n_px, px, row_line, got_line, lambda k: (at_px(k), py), line_far, 1)
+    spread_row(row, n_px, px, row_line, got_line, lambda k: (at_px(k), py), line_far, 1)
+
+    halo[6].wait_recv()
+    halo[7].wait_recv()
+    rights = edges(strips_right)
+    mine = [x[0][0] for x in solve()[0]]
+    row = collect(n_px, got_line, 1)
 
     row = jnp.broadcast_to(row, (8, 128))
     splat = [jnp.broadcast_to(row[:, k : k + 1], (8, 128)) for k in range(9)]
@@ -442,18 +496,19 @@
             pltpu.VMEM((tiles, 128), jnp.int32),
             vmem(FIELDS, 8, 128),
             vmem(FIELDS, 8, 128),
-            vmem(8, 128),
-            vmem(6, 8, 128),
+            vmem(2, 8, 128),
+            vmem(3, 8, 128),
+            vmem(3, 8, 128),
             vmem(1, 128),
             vmem(1, 128),
             vmem(n_py, 1, 128),
             vmem(n_px, 1, 128),
             dma(4),
-            dma(6),
-            dma(6),
+            dma(8),
+            dma(8),
             dma(2),
             dma(2),
-            pltpu.SemaphoreType.REGULAR((4,)),
+            pltpu.SemaphoreType.REGULAR((6,)),
         ],
         compiler_params=pltpu.CompilerParams(
             collective_id=0, has_side_effects=True, vmem_limit_bytes=8 << 20

time: 34.1 us -> 33.5 us (0.982)
  Pallas kernels: 32 us -> 31.3 us
    pallas_call x1, Pallas kernels: 32 us -> 31.3 us  [local(): pl.pallas_call(functools.partial(kernel, n_px, n_py), out_shape=[jax.Shap...]
where the time goes in v5:
time: 33.5 us; the launch traced here: 33.2 us
  Pallas kernels  31.3 us (93%)
  between operations  1.32 us (4%)
  other arithmetic  0.63 us (2%)
    pallas_call x1, Pallas kernels, local(): pl.pallas_call(functools.partial(kernel, n_px, n_py), out_shape=[jax.Shap...  31.3 us

profile of v5, /device:TPU:1, one launch (start us, length us, event | category | flops | bytes accessed | tf_op | source)
XLA Modules:
  0.0 33.2 jit_solution(4363657999424344892)
XLA Ops:
  1.3 0.0 copy-start
  1.3 0.0 copy-start.1
  1.3 31.3 %crash_step.1 = (f32[6,8,128]{2,1,0:T(8,128)S(1)}, f32[8,128]{1,0:T(8,128)S(1)}) custom-call(f32[6,8,128]{2,1,0:T(8,128)} %disp.1, f32[6,8,128]{2,1,0:T(8,128)} %force.1, f32[8,128]{1,0:T(8,128)} %mass.1, f32[8,128]{1,0:T(8,128)} %thick.1, f32[8,128]{1,0:T(8,128)} %added.1, f32[24,24]{1,0:T(8,128)} %stiff.1, s32[10,128]{1,0:T(8,128)} %elements.1, ...), custom_call_target="tpu_custom_call" | custom-call | tf_op jit(solution)/shard_map/crash_step/pallas_call | solution.py:487
  32.6 0.0 copy-done
  32.6 0.0 copy-done.1
  32.6 0.6 %multiply_add_fusion = (f32[6,8,128]{2,1,0:T(8,128)}, f32[6,8,128]{2,1,0:T(8,128)}) fusion(f32[6,8,128]{2,1,0:T(8,128)S(1)} %copy-done, f32[8,128]{1,0:T(8,128)S(1)} %get-tuple-element.5, f32[6,8,128]{2,1,0:T(8,128)S(1)} %copy-done.1, f32[6,8,128]{2,1,0:T(8,128)S(1)} %get-tuple-element.4), kind=kLoop, calls=%fused_computation | loop fusion | flops 18432 | bytes 126976 | tf_op jit(solution)/shard_map/add | solution.py:519
Async XLA Ops:
  1.3 31.3 %copy-start = (f32[6,8,128]{2,1,0:T(8,128)S(1)}, f32[6,8,128]{2,1,0:T(8,128)}, u32[]{:S(2)}) copy-start(f32[6,8,128]{2,1,0:T(8,128)} %disp.1) | copy-start | bytes 73732
  1.3 31.3 %copy-start.1 = (f32[6,8,128]{2,1,0:T(8,128)S(1)}, f32[6,8,128]{2,1,0:T(8,128)}, u32[]{:S(2)}) copy-start(f32[6,8,128]{2,1,0:T(8,128)} %param.10) | copy-start | bytes 73732

commit v6 on v5

--- a/solution.py
+++ b/solution.py
@@ -263,49 +263,30 @@
     halo[4].start()
     halo[5].start()
     plane_round(2)
-    for i in (1, 2, 4, 5):
-        halo[i].wait_recv()
-
+    halo[1].wait_recv()
+    halo[2].wait_recv()
     lower = row8 < 4
 
-    def edges(strips):
-        return strips[0], jnp.where(lower, strips[2], strips[1]), pltpu.roll(strips[2], 7, 0)
-
-    lefts = edges(strips_left)
-    rights = None
-
-    def side(i, f):
-        column = pltpu.roll(lefts[i], (128 - BASE[f] - width_of(f)) % 128, 1)
-        if rights is not None:
-            column = jnp.where(lane8 < 5, pltpu.roll(rights[i], (128 - 5 * f) % 128, 1), column)
-        return column
-
-    def extend(first, count):
-        fields = range(first, first + count)
+    def extend(beside, first, count):
+        edge = jnp.where(
+            lax.broadcasted_iota(jnp.int32, (count, 8, 128), 1) < 4,
+            below[first : first + count],
+            above[first : first + count],
+        )
+        tiles = [own[first : first + count], edge]
+        if beside is None:
+            return tiles
         return [
-            [own[first : first + count], jnp.stack([side(0, f) for f in fields])],
-            [
-                jnp.where(
-                    lax.broadcasted_iota(jnp.int32, (count, 8, 128), 1) < 4,
-                    below[first : first + count],
-                    above[first : first + count],
-                ),
-                jnp.stack([side(1, f) for f in fields]),
-            ],
+            jnp.stack([beside(i, first + c, x[c]) for c in range(count)]) for i, x in enumerate(tiles)
         ]
 
     def each(f, *xs):
-        return [[f(*[x[t][s] for x in xs]) for s in range(2)] for t in range(2)]
+        return [f(*[x[t] for x in xs]) for t in range(2)]
 
     def shift_rows(x, to, edge):
         r = each(lambda q: pltpu.roll(q, to % 8, 1), x)
-        at = lax.broadcasted_iota(jnp.int32, x[0][0].shape, 1) == edge
-        return [[jnp.where(at, r[1 - t][s], r[t][s]) for s in range(2)] for t in range(2)]
-
-    def shift_cols(x, to, edge):
-        r = each(lambda q: pltpu.roll(q, to % 128, 2), x)
-        at = lax.broadcasted_iota(jnp.int32, x[0][0].shape, 2) == edge
-        return [[jnp.where(at, r[t][1 - s], r[t][s]) for s in range(2)] for t in range(2)]
+        at = lax.broadcasted_iota(jnp.int32, x[0].shape, 1) == edge
+        return [jnp.where(at, r[1 - t], r[t]) for t in range(2)]
 
     def next_row(x):
         return shift_rows(x, -1, 7)
@@ -314,10 +295,10 @@
         return shift_rows(x, 1, 0)
 
     def next_col(x):
-        return shift_cols(x, -1, 127)
+        return each(lambda q: pltpu.roll(q, 127, 2), x)
 
     def prev_col(x):
-        return shift_cols(x, 1, 0)
+        return each(lambda q: pltpu.roll(q, 1, 2), x)
 
     def add(a, b):
         return each(lambda p, q: p + q, a, b)
@@ -330,73 +311,95 @@
         half = add(x, prev_row(x))
         return add(half, prev_col(half))
 
-    def solve():
-        u00 = extend(0, 6)
+    def solve(beside):
+        u00 = extend(beside, 0, 6)
         u01 = next_col(u00)
         u10 = next_row(u00)
+        row_12 = pltpu.roll(below[0:6], 7, 1)
+        if beside is not None:
+            row_12 = jnp.stack([beside(2, c, row_12[c]) for c in range(6)])
         at_three = lax.broadcasted_iota(jnp.int32, (6, 8, 128), 1) == 3
-        u10[1] = [
-            jnp.where(at_three, pltpu.roll(below[0:6], 7, 1), u10[1][0]),
-            jnp.where(at_three, jnp.stack([side(2, f) for f in range(6)]), u10[1][1]),
-        ]
+        u10[1] = jnp.where(at_three, row_12, u10[1])
         u11 = next_col(u10)
         corners = (u00, u01, u10, u11)
-        field_mass, field_thick, field_added = extend(12, 1), extend(13, 1), extend(14, 1)
-        forces = [[[None, None], [None, None]] for _ in range(4)]
-        for t in range(2):
-            stacked = jnp.concatenate(
-                [
-                    jnp.concatenate([corners[n][t][s][c] for c in range(6) for n in range(4)], axis=0)
-                    for s in range(2)
-                ],
-                axis=1,
-            )
-            hi = stacked.astype(BF16)
-            lo = (stacked - hi.astype(F32)).astype(BF16)
-            product = (
-                jnp.dot(big_hi, lo, preferred_element_type=F32)
-                + jnp.dot(big_lo, hi, preferred_element_type=F32)
-            ) + jnp.dot(big_hi, hi, preferred_element_type=F32)
-            for n in range(4):
-                for s in range(2):
-                    forces[n][t][s] = (
-                        jnp.stack(
-                            [
-                                product[8 * (4 * c + n) : 8 * (4 * c + n) + 8, 128 * s : 128 * s + 128]
-                                for c in range(6)
-                            ]
-                        )
-                        * field_thick[t][s]
-                    )
+        field_mass, field_thick, field_added = (extend(beside, f, 1) for f in (12, 13, 14))
+        stacked = jnp.concatenate(
+            [
+                jnp.concatenate([corners[n][t][c] for c in range(6) for n in range(4)], axis=0)
+                for t in range(2)
+            ],
+            axis=1,
+        )
+        hi = stacked.astype(BF16)
+        lo = (stacked - hi.astype(F32)).astype(BF16)
+        product = (
+            jnp.dot(big_hi, lo, preferred_element_type=F32)
+            + jnp.dot(big_lo, hi, preferred_element_type=F32)
+        ) + jnp.dot(big_hi, hi, preferred_element_type=F32)
+        forces = [
+            [
+                jnp.stack(
+                    [
+                        product[8 * (4 * c + n) : 8 * (4 * c + n) + 8, 128 * t : 128 * t + 128]
+                        for c in range(6)
+                    ]
+                )
+                * field_thick[t]
+                for t in range(2)
+            ]
+            for n in range(4)
+        ]
         internal = add(
             add(forces[0], prev_row(forces[2])), prev_col(add(forces[1], prev_row(forces[3])))
         )
-
         weight_sum = to_nodes(field_added)
         precond = each(lambda m, w: m + 0.75 * w, field_mass, weight_sum)
         inverse = each(lambda m: 1.0 / m, precond)
         quarter = each(lambda i: 0.25 * i, inverse)
         quarter_weight = each(lambda q, w: q * w, quarter, weight_sum)
-        powers = [each(lambda f, g, i: (f - g) * i, extend(6, 6), internal, inverse)]
+        powers = [
+            each(lambda f, g, i: (f - g) * i, extend(beside, 6, 6), internal, inverse)
+        ]
         for k in range(3):
             p = powers[-1]
             spread_sum = to_nodes(each(lambda a, s: a * s, field_added, four_sum(p)))
             powers.append(
                 each(lambda q, n, w, v: q * n - w * v, quarter, spread_sum, quarter_weight, p)
             )
-        return powers, precond, weight_sum, field_mass, field_thick, field_added
-
-    powers, precond, weight_sum, field_mass, field_thick, field_added = solve()
+        out = powers + [four_sum(powers[3]), precond, weight_sum, field_added, field_thick]
+        return [x[0] for x in out] + [four_sum(field_mass)[0]]
+
+    inner = solve(None)
+
     pass_on(2)
-
-    def range_of(x):
-        return jnp.where(lax.broadcasted_iota(jnp.int32, x[0][0].shape, 2) < 123, x[0][0], x[0][1])
-
-    part = [range_of(x) for x in powers]
-    mass_part, sum_part, added_part = range_of(precond), range_of(weight_sum), range_of(field_added)
+    plane_round(3)
+    halo[4].wait_recv()
+    halo[5].wait_recv()
+
+    def edges(strips):
+        return strips[0], jnp.where(lower, strips[2], strips[1]), pltpu.roll(strips[2], 7, 0)
+
+    def columns_left(tiles):
+        return lambda i, f, x: jnp.where(
+            lane8 >= 119, pltpu.roll(tiles[i], (128 - BASE[f] - width_of(f)) % 128, 1), x
+        )
+
+    def columns_right(tiles):
+        return lambda i, f, x: jnp.where(
+            lane8 < 5, pltpu.roll(tiles[i], (128 - 5 * f) % 128, 1), x
+        )
+
+    outer = solve(columns_left(edges(strips_left)))
+
+    def merge(a, b):
+        lane = lax.broadcasted_iota(jnp.int32, a.shape, 2)
+        return jnp.where((lane >= 4) & (lane < 123), a, b)
+
+    merged = [merge(a, b) for a, b in zip(inner, outer)]
+    part, last = merged[:4], merged[4]
+    mass_part, sum_part, added_part, thick_part, around_part = merged[5:]
     weighted = [mass_part * x for x in part]
     moments = [jnp.sum(weighted[k // 2] * part[k - k // 2], axis=0) for k in range(7)]
-    last = range_of(four_sum(powers[3]))
     moments.append(
         0.25 * jnp.sum(added_part * (last * last) - sum_part * (part[3] * part[3]), axis=0)
     )
@@ -405,14 +408,10 @@
     row = jnp.sum(jnp.where(row8 == lane8, sums, 0.0), axis=0, keepdims=True)
 
     added_part = added_part[0]
-    stable = 0.5 * jnp.sqrt(
-        (added_part + 0.25 * range_of(four_sum(field_mass))[0]) / range_of(field_thick)[0]
-    )
+    stable = 0.5 * jnp.sqrt((added_part + 0.25 * around_part[0]) / thick_part[0])
     smallest = jnp.min(jnp.where(added_part > 0, stable, 1e30), keepdims=True)
     lane1 = lax.broadcasted_iota(jnp.int32, (1, 128), 1)
     row = jnp.where(lane1 == 8, smallest, row)
-
-    plane_round(3)
 
     def spread_row(row, size, here, src, slots, device, far, i):
         src[...] = row
@@ -452,15 +451,16 @@
     halo[3].wait_recv()
     halo[6].start()
     halo[7].start()
-    row = collect(n_py, got_plane, 0)
     for k in range(3, rounds + 1):
         pass_on(k)
+    row = collect(n_py, got_plane, 0)
     spread_row(row, n_px, px, row_line, got_line, lambda k: (at_px(k), py), line_far, 1)
 
     halo[6].wait_recv()
     halo[7].wait_recv()
-    rights = edges(strips_right)
-    mine = [x[0][0] for x in solve()[0]]
+    beyond = solve(columns_right(edges(strips_right)))
+    lane6 = lax.broadcasted_iota(jnp.int32, (6, 8, 128), 2)
+    mine = [jnp.where(lane6 < 123, a, b) for a, b in zip(part, beyond)]
     row = collect(n_px, got_line, 1)
 
     row = jnp.broadcast_to(row, (8, 128))

time: 33.5 us -> 33.5 us (level)
  no operation moved by 1% of the time
where the time goes in v6:
time: 33.5 us; the launch traced here: 33.3 us
  Pallas kernels  31.4 us (94%)
  between operations  1.32 us (4%)
  other arithmetic  0.63 us (2%)
    pallas_call x1, Pallas kernels, local(): pl.pallas_call(functools.partial(kernel, n_px, n_py), out_shape=[jax.Shap...  31.4 us

profile of v6, /device:TPU:1, one launch (start us, length us, event | category | flops | bytes accessed | tf_op | source)
XLA Modules:
  0.0 33.3 jit_solution(7803811289599640515)
XLA Ops:
  1.3 0.0 copy-start
  1.3 0.0 copy-start.1
  1.3 31.4 %crash_step.1 = (f32[6,8,128]{2,1,0:T(8,128)S(1)}, f32[8,128]{1,0:T(8,128)S(1)}) custom-call(f32[6,8,128]{2,1,0:T(8,128)} %disp.1, f32[6,8,128]{2,1,0:T(8,128)} %force.1, f32[8,128]{1,0:T(8,128)} %mass.1, f32[8,128]{1,0:T(8,128)} %thick.1, f32[8,128]{1,0:T(8,128)} %added.1, f32[24,24]{1,0:T(8,128)} %stiff.1, s32[10,128]{1,0:T(8,128)} %elements.1, ...), custom_call_target="tpu_custom_call" | custom-call | tf_op jit(solution)/shard_map/crash_step/pallas_call | solution.py:487
  32.7 0.0 copy-done
  32.7 0.0 copy-done.1
  32.7 0.6 %multiply_add_fusion = (f32[6,8,128]{2,1,0:T(8,128)}, f32[6,8,128]{2,1,0:T(8,128)}) fusion(f32[6,8,128]{2,1,0:T(8,128)S(1)} %copy-done, f32[8,128]{1,0:T(8,128)S(1)} %get-tuple-element.5, f32[6,8,128]{2,1,0:T(8,128)S(1)} %copy-done.1, f32[6,8,128]{2,1,0:T(8,128)S(1)} %get-tuple-element.4), kind=kLoop, calls=%fused_computation | loop fusion | flops 18432 | bytes 126976 | tf_op jit(solution)/shard_map/add | solution.py:519
Async XLA Ops:
  1.3 31.4 %copy-start = (f32[6,8,128]{2,1,0:T(8,128)S(1)}, f32[6,8,128]{2,1,0:T(8,128)}, u32[]{:S(2)}) copy-start(f32[6,8,128]{2,1,0:T(8,128)} %disp.1) | copy-start | bytes 73732
  1.3 31.4 %copy-start.1 = (f32[6,8,128]{2,1,0:T(8,128)S(1)}, f32[6,8,128]{2,1,0:T(8,128)}, u32[]{:S(2)}) copy-start(f32[6,8,128]{2,1,0:T(8,128)} %param.10) | copy-start | bytes 73732
